TPU v7x, 256 devices: a whole 4x4x8 slice. The times are simulated.
256 devices in a mesh: outer: 4 (over x), inner: 16 (over z_hi, y), tensor: 4 (over z_lo, core).
Axes of the slice: x: 4, y: 4, z: 8 (z_hi: 4, z_lo: 2; z = z_hi * 2 + z_lo), core: 2. Of those that a mesh axis runs over, the one named last changes fastest.
Arguments:
- hidden_in: bfloat16 [12288, 4096], P(('outer', 'inner', 'tensor')), may hold values from -15 to 15
- norm_gain: float32 [4096], replicated, may hold values from 0.5 to 5
- w_query: bfloat16 [4096, 4096], P('inner', 'tensor'), may hold values from -0.110485435 to 0.110485435
- w_key: bfloat16 [4096, 1024], P('inner', 'tensor'), may hold values from -0.110485435 to 0.110485435
- value_weight: bfloat16 [4096, 1024], P('inner', 'tensor'), may hold values from -0.09375 to 0.09375
- w_out: bfloat16 [4096, 4096], P('tensor'), may hold values from -0.09375 to 0.09375
- doc_ids: int32 [12288], P(('outer', 'inner')), may hold values from 0 to 5, as said below
- positions: int32 [12288], P(('outer', 'inner')), may hold values from 0 to 65535, as said below
Outputs:
- layer_out: bfloat16 [12288, 4096], P(('outer', 'inner', 'tensor'))
Inputs may be any that keep to these rules, and one draw needn't show every extreme that they name: `doc_ids`: document numbers never fall along the sequence; each of the 6 documents has at least one token, and exactly one of them has 7680 tokens. Document numbers may be sent packed or coded. `positions`: inside a document the position rises by one from each token to the next; one document other than the one of 7680 tokens ends at position 65535.
All inputs are finite; a program needn't handle non-finite values.
Results may differ from a plain program's by a relative error of at most 0.012.
The roundings to bfloat16 on the way count: a program that leaves them out, or rounds other values in their place, can miss the bound.
Values may be sent and summed in bfloat16 or wider, within the bound.
A program may use at most 128 MiB of HBM per device.

v0:
```python
import math

import jax
import jax.numpy as jnp
from jax import lax
from jax.sharding import PartitionSpec as P

HEAD_SIZE = 128


rope_base = 500000.0
yarn_factor = 8.0
trained_context = 8192.0
beta_fast = 32.0
beta_slow = 1.0
norm_epsilon = 1e-05
masked_score = -1e30


def yarn_inverse(head_dim):
    half_dim = head_dim // 2

    def correction(rotations):
        return (
            head_dim
            * math.log(trained_context / (rotations * 2.0 * math.pi))
            / (2.0 * math.log(rope_base))
        )

    lowest = max(math.floor(correction(beta_fast)), 0)
    highest = min(math.ceil(correction(beta_slow)), head_dim - 1)
    spread = max(highest - lowest, 0.001)
    values = []
    for column in range(half_dim):
        extrapolated = rope_base ** (-2.0 * column / head_dim)
        ramp = min(max((column - lowest) / spread, 0.0), 1.0)
        values.append(extrapolated / yarn_factor * ramp + extrapolated * (1.0 - ramp))
    return values


def yarn_tables(positions, head_dim):
    inverse = jnp.asarray(yarn_inverse(head_dim), dtype=jnp.float32)
    attention_gain = 0.1 * math.log(yarn_factor) + 1.0
    angles = positions.astype(jnp.float32)[:, None] * inverse[None, :]
    return (jnp.cos(angles) * attention_gain, jnp.sin(angles) * attention_gain)


def apply_rotation(heads, cosine_table, sine_table):
    half_dim = heads.shape[-1] // 2
    first_half = heads[..., :half_dim]
    second_half = heads[..., half_dim:]
    cos_rows = cosine_table[:, None, :]
    sin_rows = sine_table[:, None, :]
    return jnp.concatenate(
        [
            first_half * cos_rows - second_half * sin_rows,
            second_half * cos_rows + first_half * sin_rows,
        ],
        axis=-1,
    )


def rms_normed(hidden_in, norm_gain):
    widened = hidden_in.astype(jnp.float32)
    power = jnp.mean(widened * widened, axis=-1, keepdims=True)
    return (widened * lax.rsqrt(power + norm_epsilon) * norm_gain).astype(jnp.bfloat16)


def body(hidden_in, norm_gain, w_query, w_key, value_weight, w_out, doc_ids, positions):
    normed = rms_normed(hidden_in, norm_gain)
    block_rows = lax.all_gather(normed, "tensor", axis=0, tiled=True)
    tokens_here = block_rows.shape[0]
    query_width = w_query.shape[1]
    key_width = w_key.shape[1]
    pieces = (
        lax.all_gather(w_query, "inner", axis=0, tiled=True),
        lax.all_gather(w_key, "inner", axis=0, tiled=True),
        lax.all_gather(value_weight, "inner", axis=0, tiled=True),
    )
    queries, key_matrix, value_matrix = tuple(
        (
            jnp.dot(block_rows, weight_piece, preferred_element_type=jnp.float32)
            for weight_piece in pieces
        )
    )
    value_matrix = value_matrix.astype(jnp.bfloat16)
    heads_query = query_width // HEAD_SIZE
    heads_key = key_width // HEAD_SIZE
    queries_per_group = heads_query // heads_key
    cosine_table, sine_table = yarn_tables(positions, HEAD_SIZE)
    query_rot = (
        apply_rotation(
            queries.reshape(tokens_here, heads_query, HEAD_SIZE), cosine_table, sine_table
        )
        .astype(jnp.bfloat16)
        .reshape(tokens_here, query_width)
    )
    rotated_keys = (
        apply_rotation(
            key_matrix.reshape(tokens_here, heads_key, HEAD_SIZE), cosine_table, sine_table
        )
        .astype(jnp.bfloat16)
        .reshape(tokens_here, key_width)
    )
    documents = lax.all_gather(doc_ids, ("outer", "inner"), axis=0, tiled=True)
    length_all = documents.shape[0]
    block_index = lax.axis_index(("outer", "inner"))
    sequence_index = jnp.arange(length_all, dtype=jnp.int32)
    query_documents = lax.dynamic_slice_in_dim(documents, block_index * tokens_here, tokens_here, 0)
    query_index = lax.dynamic_slice_in_dim(
        sequence_index, block_index * tokens_here, tokens_here, 0
    )
    row_documents = jnp.tile(query_documents, queries_per_group)
    row_index = jnp.tile(query_index, queries_per_group)
    top_index = jnp.max(query_index)
    top_document = jnp.max(query_documents)
    low_document = jnp.min(query_documents)
    grouped_heads = jnp.transpose(
        query_rot.reshape(tokens_here, heads_key, queries_per_group, HEAD_SIZE), (1, 2, 0, 3)
    ).reshape(heads_key, queries_per_group * tokens_here, HEAD_SIZE)
    score_scale = HEAD_SIZE ** (-0.5)

    def key_block(running, block_keys, block_values, first_row):
        row_count = block_keys.shape[0]
        piece_index = lax.dynamic_slice_in_dim(sequence_index, first_row, row_count, 0)
        piece_documents = lax.dynamic_slice_in_dim(documents, first_row, row_count, 0)
        live = (
            (jnp.min(piece_index) <= top_index)
            & (jnp.min(piece_documents) <= top_document)
            & (jnp.max(piece_documents) >= low_document)
        )

        def attend(current):
            row_peaks, totals, summed = current
            heads_keys = block_keys.reshape(row_count, heads_key, HEAD_SIZE)
            heads_values = block_values.reshape(row_count, heads_key, HEAD_SIZE)
            scores = (
                jnp.einsum(
                    "hqd,khd->hqk", grouped_heads, heads_keys, preferred_element_type=jnp.float32
                )
                * score_scale
            )
            allowed = (row_index[:, None] >= piece_index[None, :]) & (
                row_documents[:, None] == piece_documents[None, :]
            )
            scores = jnp.where(allowed[None], scores, masked_score)
            fresh = jnp.maximum(row_peaks, jnp.max(scores, axis=-1))
            weights = jnp.where(allowed[None], jnp.exp(scores - fresh[..., None]), 0.0)
            shrink = jnp.exp(row_peaks - fresh)
            totals = totals * shrink + jnp.sum(weights, axis=-1)
            summed = summed * shrink[..., None] + jnp.einsum(
                "hqk,khd->hqd",
                weights.astype(jnp.bfloat16),
                heads_values,
                preferred_element_type=jnp.float32,
            )
            return (fresh, totals, summed)

        return lax.cond(live, attend, lambda current: current, running)

    initial = (
        jnp.full((heads_key, queries_per_group * tokens_here), masked_score, jnp.float32),
        jnp.zeros((heads_key, queries_per_group * tokens_here), jnp.float32),
        jnp.zeros((heads_key, queries_per_group * tokens_here, HEAD_SIZE), jnp.float32),
    )
    piece_keys = lax.all_gather(rotated_keys, ("outer", "inner"), axis=0, tiled=True)
    piece_values = lax.all_gather(value_matrix, ("outer", "inner"), axis=0, tiled=True)
    row_count = piece_keys.shape[0]
    step_rows = 512
    steps_count = row_count // step_rows
    split_keys = piece_keys.reshape(steps_count, step_rows, key_width)
    split_values = piece_values.reshape(steps_count, step_rows, key_width)
    offsets = jnp.arange(steps_count, dtype=jnp.int32) * step_rows

    def scan_step(current, inputs):
        block_keys, block_values, offset = inputs
        return (key_block(current, block_keys, block_values, offset), None)

    result, unused = lax.scan(scan_step, initial, (split_keys, split_values, offsets))
    row_peaks, totals, summed = result
    heads_out = (summed / totals[..., None]).astype(jnp.bfloat16)
    attended = jnp.transpose(
        heads_out.reshape(heads_key, queries_per_group, tokens_here, HEAD_SIZE), (2, 0, 1, 3)
    ).reshape(tokens_here, query_width)
    full_term = jnp.dot(attended, w_out, preferred_element_type=jnp.float32)
    projected = lax.psum_scatter(
        full_term.astype(jnp.bfloat16), "tensor", scatter_dimension=0, tiled=True
    ).astype(jnp.float32)
    return (hidden_in.astype(jnp.float32) + projected).astype(jnp.bfloat16)


def solution(mesh):
    in_specs = (
        P(("outer", "inner", "tensor"), None),
        P(),
        P("inner", "tensor"),
        P("inner", "tensor"),
        P("inner", "tensor"),
        P("tensor", None),
        P(("outer", "inner")),
        P(("outer", "inner")),
    )
    out_specs = P(("outer", "inner", "tensor"), None)
    return jax.shard_map(body, mesh=mesh, in_specs=in_specs, out_specs=out_specs, check_vma=False)
```

profile of v0, /device:TPU:46, one launch (start us, length us, event | category | flops | bytes accessed | tf_op | source)
XLA Modules:
  0.0 824.8 jit_solution(2318487250377459623)
XLA Ops:
  6.5 1.2 fusion.16
  7.7 1.9 fusion.18
  9.7 0.7 all-gather.9.cloned.1.call-update
  10.5 0.7 all-gather.15.cloned.1.call-update
  11.8 0.7 convert_element_type.42
  12.5 1.1 fusion.20
  13.5 24.8 %all-gather.7.cloned.1.call-done = bf16[192,4096]{1,0:T(8,128)(2,1)} async-done(((bf16[48,4096]{1,0:T(8,128)(2,1)}), bf16[192,4096]{1,0:T(8,128)(2,1)}) %all-gather.7.cloned.1.call-update) | async-done | bytes 1572880 | tf_op jit(solution)/shard_map/all_gather | solution.py:71
  38.3 61.6 %all-gather.9.cloned.1.call-done = bf16[4096,256]{1,0:T(8,128)(2,1)} async-done(((bf16[256,256]{1,0:T(8,128)(2,1)}), bf16[4096,256]{1,0:T(8,128)(2,1)}) %all-gather.9.cloned.1.call-update) | async-done | bytes 2097168 | tf_op jit(solution)/shard_map/all_gather | solution.py:77
  99.9 2.6 fusion.26
  103.4 0.7 copy.36
  104.2 55.5 %all-gather.15.cloned.1.call-done = bf16[4096,256]{1,0:T(8,128)(2,1)} async-done(((bf16[256,256]{1,0:T(8,128)(2,1)}), bf16[4096,256]{1,0:T(8,128)(2,1)}) %all-gather.15.cloned.1.call-update) | async-done | bytes 2097168 | tf_op jit(solution)/shard_map/all_gather | solution.py:78
  159.7 2.8 convolution_convert_fusion.1
  162.6 0.7 dynamic-slice
  164.2 352.3 %all-reduce = s32[12288]{0:T(1024)S(1)} all-reduce(s32[12288]{0:T(1024)S(1)} %dynamic-update-slice), channel_id=1, replica_groups=mesh['outer'=4,'inner'=16,'tensor'=4] {'outer','inner'}, use_global_device_ids=true, to_apply=%add | all-reduce | flops 12288 | bytes 98304
  516.5 0.7 iota_add_fusion
  517.2 0.8 fusion.24
  518.0 5.2 convolution_bitcast_fusion
  524.2 8.6 %copy.25 = bf16[24,512,256]{1,2,0:T(8,128)(2,1)} copy(bf16[24,512,256]{2,1,0:T(8,128)(2,1)} %bitcast.52) | data formatting | bytes 12582912
  532.8 8.6 %copy.26 = bf16[24,512,256]{1,2,0:T(8,128)(2,1)} copy(bf16[24,512,256]{2,1,0:T(8,128)(2,1)} %bitcast.53) | data formatting | bytes 12582912
  541.5 181.7 %while.15 = (s32[]{:T(128)}, f32[2,768]{1,0:T(2,128)S(1)}, f32[2,768]{1,0:T(2,128)S(1)}, f32[2,768,128]{2,1,0:T(8,128)S(1)}, s32[24]{0:T(128)S(1)}, /*index=5*/s...) while((s32[]{:T(128)}, f32[2,768]{1,0:T(2,128)S(1)}, ...), condition=%wide.region_12.13_spmd.clone, body=%wide.region_4.12_spmd.clone.sunk | while | flops 414454272 | bytes 14686109 | solution.py:179
  541.5 0.6 dynamic_slice.46
  544.1 0.8 fusion.39
  548.7 0.6 dynamic_slice.46
  551.2 0.8 fusion.39
  555.9 0.6 dynamic_slice.46
  558.4 0.8 fusion.39
  563.0 0.6 dynamic_slice.46
  565.6 0.8 fusion.39
  570.2 0.6 dynamic_slice.46
  572.7 0.8 fusion.39
  577.4 0.6 dynamic_slice.46
  579.9 0.8 fusion.39
  587.1 0.8 fusion.39
  594.2 0.8 fusion.39
  601.4 0.8 fusion.39
  608.6 0.8 fusion.39
  615.7 0.8 fusion.39
  622.9 0.8 fusion.39
  630.0 0.8 fusion.39
  634.7 0.6 dynamic_slice.46
  637.2 0.8 fusion.39
  644.4 0.8 fusion.39
  651.5 0.8 fusion.39
  658.7 0.8 fusion.39
  665.9 0.8 fusion.39
  670.5 4.9 conditional.3
  671.0 1.1 constant_dynamic-slice_fusion
  672.1 0.9 fusion.4
  673.0 0.8 fusion.6
  673.9 1.5 fusion.10
  677.9 0.8 fusion.39
  682.5 4.9 conditional.3
  683.1 1.1 constant_dynamic-slice_fusion
  684.2 0.9 fusion.4
  685.1 0.8 fusion.6
  685.9 1.5 fusion.10
  690.0 0.8 fusion.39
  697.1 0.8 fusion.39
  704.3 0.8 fusion.39
  711.5 0.8 fusion.39
  718.6 0.8 fusion.39
  724.2 6.4 convolution_convert_fusion
  730.6 85.5 %reduce-scatter.2.cloned.1.call-done = bf16[48,4096]{1,0:T(8,128)(2,1)} async-done(((bf16[192,4096]{1,0:T(8,128)(2,1)}), bf16[48,4096]{1,0:T(8,128)(2,1)}) %reduce-scatter.2.cloned.1.call-update) | async-done | bytes 393232 | tf_op jit(solution)/shard_map/reduce_scatter | solution.py:186
  816.1 1.8 fusion.19
  (97 shorter events, 15.1 us)
Async XLA Ops:
  6.5 31.8 %all-gather.7.cloned.1.call-start = ((), (), s32[]{:S(2)}) async-start(), calls=%async_computation.1 | async-start | bytes 1966080 | tf_op jit(solution)/shard_map/all_gather | solution.py:71
  9.7 90.3 %all-gather.9.cloned.1.call-start = ((), (), s32[]{:S(2)}) async-start(), calls=%async_computation.2 | async-start | bytes 2228224 | tf_op jit(solution)/shard_map/all_gather | solution.py:77
  10.4 149.2 %all-gather.15.cloned.1.call-start = ((), (), s32[]{:S(2)}) async-start(), calls=%async_computation.5 | async-start | bytes 2228224 | tf_op jit(solution)/shard_map/all_gather | solution.py:78
  11.1 506.9 %all-gather.13.cloned.1.call-start = ((), (), s32[]{:S(2)}) async-start(), calls=%async_computation.4 | async-start | bytes 8912896 | tf_op jit(solution)/shard_map/all_gather | solution.py:76
  11.7 512.4 %all-gather.11.cloned.1.call-start = ((), (), s32[]{:S(2)}) async-start(), calls=%async_computation.3 | async-start | bytes 6389760 | tf_op jit(solution)/shard_map/all_gather | solution.py:166
  38.3 121.3 %copy-start.1 = (bf16[192,4096]{1,0:T(8,128)(2,1)S(1)}, bf16[192,4096]{1,0:T(8,128)(2,1)}, u32[]{:S(2)}) copy-start(bf16[192,4096]{1,0:T(8,128)(2,1)} %all-gather.7.cloned.1.call-done) | copy-start | bytes 4718596
  102.6 59.9 %copy-start.3 = (u32[256]{0:T(256)S(1)}, u32[256]{0:T(256)}, u32[]{:S(2)}) copy-start(u32[256]{0:T(256)} %constant.82) | copy-start | bytes 3076
  102.6 61.3 %copy-start.2 = (s32[192]{0:T(256)S(1)}, s32[192]{0:T(256)}, u32[]{:S(2)}) copy-start(s32[192]{0:T(256)} %param.19) | copy-start | bytes 2308
  104.1 428.7 %all-gather.17.cloned.1.call-start = ((), (), s32[]{:S(2)}) async-start(), calls=%async_computation.6 | async-start | bytes 6389760 | tf_op jit(solution)/shard_map/all_gather | solution.py:167
  162.5 653.6 %reduce-scatter.2.cloned.1.call-start = ((), (), s32[]{:S(2)}) async-start(), calls=%async_computation.7 | async-start | bytes 1966080 | tf_op jit(solution)/shard_map/reduce_scatter | solution.py:186
  724.1 91.9 %copy-start = (bf16[48,4096]{1,0:T(8,128)(2,1)S(1)}, bf16[48,4096]{1,0:T(8,128)(2,1)}, u32[]{:S(2)}) copy-start(bf16[48,4096]{1,0:T(8,128)(2,1)} %param.13) | copy-start | bytes 1179652
Sparse Core Ops, SparseCore 0:
  9.8 28.5 all-gather.6
  40.8 59.1 all-gather.8
  102.4 57.2 all-gather.14
  161.9 117.3 all-gather.12
  282.4 100.1 all-gather.10
  385.8 99.9 all-gather.16
  730.7 85.3 reduce-scatter.1
where the time goes:
time: 830 us; the launch traced here: 825 us
  blocking collectives  352 us (42%)
  waiting for transfers between devices  229 us (28%)
  loops' own time  138 us (17%)
  local copies, waits for them, and re-layouts  36.5 us (4%)
  other arithmetic  31.7 us (4%)
  matrix products  21.7 us (3%)
  between operations  14.4 us (2%)
    unnamed x1, blocking collectives  352 us
    another operation x1, loops' own time, body(): lax.scan(scan_step, initial, (split_keys, split_values, offsets))  138 us
    reduce_scatter x1, waiting for transfers between devices, body(): lax.psum_scatter(full_term.astype(jnp.bfloat16), 'tensor', scatter_dimens...  85.5 us
    all_gather x1, waiting for transfers between devices, body(): lax.all_gather(w_key, 'inner', axis=0, tiled=True)  61.6 us
    all_gather x1, waiting for transfers between devices, body(): lax.all_gather(value_weight, 'inner', axis=0, tiled=True)  55.5 us
    all_gather x1, waiting for transfers between devices, body(): block_rows = lax.all_gather(normed, 'tensor', axis=0, tiled=True)  24.8 us
    reduce_max x24, other arithmetic, key_block(): jnp.max(piece_documents) >= low_document  19.5 us
    unnamed x15, local copies, waits for them, and re-layouts  19.1 us
  transfers between devices with their start and end apart: 7, of which 4 were waited for; matrix products, arithmetic and copies ran while one was open for 3% of the time, Pallas kernels for 0%

commit v1 on v0

v1 whole, which is shorter than its diff:
```python
import functools
import math

import jax
import jax.numpy as jnp
from jax import lax
from jax.experimental import pallas as pl
from jax.experimental.pallas import tpu as pltpu
from jax.sharding import PartitionSpec as P

HEAD_SIZE = 128
BLOCK = 192
SEQUENCE = 12288
KEY_TILE = 512
MESH = pl.DeviceIdType.MESH


rope_base = 500000.0
yarn_factor = 8.0
trained_context = 8192.0
beta_fast = 32.0
beta_slow = 1.0
norm_epsilon = 1e-05
masked_score = -1e30


def yarn_inverse(head_dim):
    half_dim = head_dim // 2

    def correction(rotations):
        return (
            head_dim
            * math.log(trained_context / (rotations * 2.0 * math.pi))
            / (2.0 * math.log(rope_base))
        )

    lowest = max(math.floor(correction(beta_fast)), 0)
    highest = min(math.ceil(correction(beta_slow)), head_dim - 1)
    spread = max(highest - lowest, 0.001)
    values = []
    for column in range(half_dim):
        extrapolated = rope_base ** (-2.0 * column / head_dim)
        ramp = min(max((column - lowest) / spread, 0.0), 1.0)
        values.append(extrapolated / yarn_factor * ramp + extrapolated * (1.0 - ramp))
    return values


def yarn_tables(positions, head_dim):
    inverse = jnp.asarray(yarn_inverse(head_dim), dtype=jnp.float32)
    attention_gain = 0.1 * math.log(yarn_factor) + 1.0
    angles = positions.astype(jnp.float32)[:, None] * inverse[None, :]
    return (jnp.cos(angles) * attention_gain, jnp.sin(angles) * attention_gain)


def apply_rotation(heads, cosine_table, sine_table):
    half_dim = heads.shape[-1] // 2
    first_half = heads[..., :half_dim]
    second_half = heads[..., half_dim:]
    cos_rows = cosine_table[:, None, :]
    sin_rows = sine_table[:, None, :]
    return jnp.concatenate(
        [
            first_half * cos_rows - second_half * sin_rows,
            second_half * cos_rows + first_half * sin_rows,
        ],
        axis=-1,
    )


def rms_normed(hidden_in, norm_gain):
    widened = hidden_in.astype(jnp.float32)
    power = jnp.mean(widened * widened, axis=-1, keepdims=True)
    return (widened * lax.rsqrt(power + norm_epsilon) * norm_gain).astype(jnp.bfloat16)


def place():
    outer, inner, tensor = (lax.axis_index(name) for name in ("outer", "inner", "tensor"))
    return outer, inner % 4, inner // 4, tensor // 2, tensor % 2


def device(x, y, zh, zl, c):
    return (x, zh * 4 + y, zl * 2 + c)


def greet(partners):
    barrier = pltpu.get_barrier_semaphore()
    for partner in partners:
        pl.semaphore_signal(barrier, inc=1, device_id=partner, device_id_type=MESH)
    pl.semaphore_wait(barrier, len(partners))


class Copies:
    def __init__(self, send_sems, recv_sems):
        self.send_sems, self.recv_sems, self.count, self.sent = send_sems, recv_sems, 0, []

    def send(self, src, dst, target):
        copy = pltpu.make_async_remote_copy(
            src_ref=src,
            dst_ref=dst,
            send_sem=self.send_sems.at[self.count],
            recv_sem=self.recv_sems.at[self.count],
            device_id=target,
            device_id_type=MESH,
        )
        self.count += 1
        copy.start()
        self.sent.append(copy)
        return copy

    def finish(self):
        for copy in self.sent:
            copy.wait_send()


def gather_kernel(
    normed, weights, meta, rows_out, weights_out, meta_out, send_sems, recv_sems, a2a_send, a2a_recv, local_sems
):
    x, y, zh, zl, c = place()
    p = zh * 2 + zl
    near = lambda q: device(x, y, (q % 8) // 2, q % 2, c)
    right, left = near(p + 1), near(p + 7)
    sibling = device(x, y, zh, zl, 1 - c)
    y_next, y_prev = device(x, (y + 1) % 4, zh, zl, c), device(x, (y + 3) % 4, zh, zl, c)
    x_next, x_prev = device((x + 1) % 4, y, zh, zl, c), device((x + 3) % 4, y, zh, zl, c)
    y_far, x_far = device(x, (y + 2) % 4, zh, zl, c), device((x + 2) % 4, y, zh, zl, c)
    columns = [device(x, y, (zh + k) % 4, zl, cc) for k in range(4) for cc in (c, 1 - c)][1:]
    greet(columns + [right, left, y_next, y_prev, y_far, x_next, x_prev, x_far])
    cp = Copies(send_sems, recv_sems)

    a2a = []
    for j in range(2):
        for cc in range(2):
            zt = 2 * c + j
            own = (zt == zh) & (c == cc)
            copy = pltpu.make_async_remote_copy(
                src_ref=weights.at[2 * j + cc],
                dst_ref=weights_out.at[zh, y, x],
                send_sem=a2a_send.at[2 * j + cc],
                recv_sem=a2a_recv.at[zh],
                device_id=device(x, y, zt, zl, cc),
                device_id_type=MESH,
            )
            stay = pltpu.make_async_copy(
                weights.at[2 * j + cc], weights_out.at[zh, y, x], local_sems.at[0]
            )
            pl.when(own)(stay.start)
            pl.when(jnp.logical_not(own))(copy.start)
            a2a.append((own, copy, stay))
    own_row = pltpu.make_async_copy(normed, rows_out.at[p, c], local_sems.at[1])
    own_row.start()
    own_meta = pltpu.make_async_copy(meta, meta_out.at[x, y, zh], local_sems.at[2])
    own_meta.start()

    to_right, to_left, to_sibling = {}, {}, []
    for h in range(2):
        spot = rows_out.at[p, c, h]
        to_right[0, h] = cp.send(normed.at[h], spot, right)
        to_left[0, h] = cp.send(normed.at[h], spot, left)
    to_sibling.append(cp.send(normed, rows_out.at[p, c], sibling))
    meta_z = [
        cp.send(meta, meta_out.at[x, y, zh], device(x, y, (zh + k) % 4, zl, c)) for k in (1, 2, 3)
    ]

    for source in range(4):
        arrives = pltpu.make_async_remote_copy(
            src_ref=weights.at[0],
            dst_ref=weights_out.at[source, y, x],
            send_sem=a2a_send.at[0],
            recv_sem=a2a_recv.at[source],
            device_id=sibling,
            device_id_type=MESH,
        )
        own = (zh == source) & (c == zh // 2)
        pl.when(jnp.logical_not(own))(arrives.wait_recv)
    for own, copy, stay in a2a:
        pl.when(own)(stay.wait)
    mine = weights_out.at[:, y, x]
    wy_next, wy_prev = cp.send(mine, mine, y_next), cp.send(mine, mine, y_prev)
    wx = {}

    def along_x(yy):
        piece = weights_out.at[:, yy, x]
        wx[len(wx)] = (yy, cp.send(piece, piece, x_next), cp.send(piece, piece, x_prev))

    forwards = []

    def forward_x(k):
        yy, a, b = wx[k]
        a.wait_recv()
        piece = weights_out.at[pl.ds(0, 2), yy, (x + 3) % 4]
        forwards.append(cp.send(piece, piece, x_next))
        b.wait_recv()
        piece = weights_out.at[pl.ds(2, 2), yy, (x + 1) % 4]
        forwards.append(cp.send(piece, piece, x_prev))

    along_x(y)
    own_meta.wait()
    for copy in meta_z:
        copy.wait_recv()
    mine = meta_out.at[x, y]
    meta_y = [cp.send(mine, mine, device(x, (y + k) % 4, zh, zl, c)) for k in (1, 2, 3)]

    def ring(step):
        for h in range(2):
            if (step, h) in to_right:
                to_right[step, h].wait_recv()
                spot = rows_out.at[(p + 7 - step) % 8, c, h]
                if step < 2 or (step == 2 and h == 0):
                    to_right[step + 1, h] = cp.send(spot, spot, right)
                to_sibling.append(cp.send(spot, spot, sibling))
            if (step, h) in to_left:
                to_left[step, h].wait_recv()
                spot = rows_out.at[(p + 1 + step) % 8, c, h]
                if step < 2 or (step == 2 and h == 1):
                    to_left[step + 1, h] = cp.send(spot, spot, left)
                to_sibling.append(cp.send(spot, spot, sibling))

    ring(0)
    wy_next.wait_recv()
    piece = weights_out.at[pl.ds(0, 2), (y + 3) % 4, x]
    wy_far_next = cp.send(piece, piece, y_next)
    along_x((y + 3) % 4)
    wy_prev.wait_recv()
    piece = weights_out.at[pl.ds(2, 2), (y + 1) % 4, x]
    wy_far_prev = cp.send(piece, piece, y_prev)
    along_x((y + 1) % 4)
    for copy in meta_y:
        copy.wait_recv()
    mine = meta_out.at[x]
    meta_x = [cp.send(mine, mine, device((x + k) % 4, y, zh, zl, c)) for k in (1, 2, 3)]
    forward_x(0)
    wy_far_next.wait_recv()
    wy_far_prev.wait_recv()
    along_x((y + 2) % 4)
    ring(1)
    forward_x(1)
    forward_x(2)
    ring(2)
    forward_x(3)
    ring(3)
    for copy in forwards + to_sibling + meta_x:
        copy.wait_recv()
    own_row.wait()
    for own, copy, stay in a2a:
        pl.when(jnp.logical_not(own))(copy.wait_send)
    cp.finish()


def gather(normed, weights, meta):
    anywhere = pl.BlockSpec(memory_space=pl.ANY)
    return pl.pallas_call(
        gather_kernel,
        out_shape=(
            jax.ShapeDtypeStruct((8, 2, 2, 24, 4096), jnp.bfloat16),
            jax.ShapeDtypeStruct((4, 4, 4, 64, 384), jnp.bfloat16),
            jax.ShapeDtypeStruct((4, 4, 4, 8, 128), jnp.int32),
        ),
        in_specs=[anywhere] * 3,
        out_specs=(anywhere,) * 3,
        scratch_shapes=[
            pltpu.SemaphoreType.DMA((64,)),
            pltpu.SemaphoreType.DMA((64,)),
            pltpu.SemaphoreType.DMA((4,)),
            pltpu.SemaphoreType.DMA((4,)),
            pltpu.SemaphoreType.DMA((3,)),
        ],
        compiler_params=pltpu.CompilerParams(collective_id=0, has_side_effects=True),
        name="gather",
    )(normed, weights, meta)


def keys_kernel(own, out, send_sems, recv_sems, local_sem):
    x, y, zh, zl, c = place()
    sibling = device(x, y, zh, zl, 1 - c)
    xs = [(x + k) % 4 for k in range(4)]
    ys = [(y + k) % 4 for k in range(4)]
    y_next, y_prev = device(x, ys[1], zh, zl, c), device(x, ys[3], zh, zl, c)
    x_next, x_prev = device(xs[1], y, zh, zl, c), device(xs[3], y, zh, zl, c)
    greet([sibling, y_next, y_prev, x_next, x_prev])
    cp = Copies(send_sems, recv_sems)
    whole = lambda xx, yy: out.at[c, xx, :, :, yy]
    half = lambda f, xx, yy: out.at[c, xx, f, :, yy]
    part = lambda a, xx, yy: out.at[c, xx, :, a, yy]
    cell = lambda f, a, xx, yy: out.at[c, xx, f, a, yy]
    same = lambda ref, target: cp.send(ref, ref, target)

    stay = pltpu.make_async_copy(own, whole(x, y), local_sem.at[0])
    stay.start()
    from_y_prev = cp.send(own, whole(x, y), y_next)
    from_y_next = cp.send(own, whole(x, y), y_prev)
    from_x_prev = cp.send(own, whole(x, y), x_next)
    from_x_next = cp.send(own, whole(x, y), x_prev)
    siblings = [cp.send(own, whole(x, y), sibling)]

    def share(xx, yy):
        siblings.append(same(whole(xx, yy), sibling))

    a_prev, a_next, b_prev, b_next = {}, {}, {}, {}

    def a_send(k):
        a_prev[k] = same(part(0, x, ys[k]), x_next)
        a_next[k] = same(part(0, x, ys[k]), x_prev)

    def b_send(k):
        b_prev[k] = same(part(1, xs[k], y), y_next)
        b_next[k] = same(part(1, xs[k], y), y_prev)

    from_y_prev.wait_recv()
    y_far_prev = same(half(0, x, ys[3]), y_next)
    a_send(3)
    from_x_prev.wait_recv()
    x_far_prev = same(half(0, xs[3], y), x_next)
    b_send(3)
    from_y_next.wait_recv()
    y_far_next = same(half(1, x, ys[1]), y_prev)
    a_send(1)
    from_x_next.wait_recv()
    x_far_next = same(half(1, xs[1], y), x_prev)
    b_send(1)
    share(x, ys[3])
    share(x, ys[1])
    share(xs[3], y)
    share(xs[1], y)
    y_far_prev.wait_recv()
    y_far_next.wait_recv()
    a_send(2)
    x_far_prev.wait_recv()
    x_far_next.wait_recv()
    b_send(2)
    share(x, ys[2])
    share(xs[2], y)
    fa, fb = {}, {}
    for k in (3, 1, 2):
        a_prev[k].wait_recv()
        fa[k, 0] = same(cell(0, 0, xs[3], ys[k]), x_next)
        b_prev[k].wait_recv()
        fb[k, 0] = same(cell(0, 1, xs[k], ys[3]), y_next)
        a_next[k].wait_recv()
        fa[k, 1] = same(cell(1, 0, xs[1], ys[k]), x_prev)
        b_next[k].wait_recv()
        fb[k, 1] = same(cell(1, 1, xs[k], ys[1]), y_prev)
        if k == 1:
            for xx in (1, 3):
                for yy in (1, 3):
                    share(xs[xx], ys[yy])
    for k in (3, 1, 2):
        for f in range(2):
            fa[k, f].wait_recv()
            fb[k, f].wait_recv()
        if k == 2:
            share(xs[1], ys[2])
            share(xs[3], ys[2])
            share(xs[2], ys[1])
            share(xs[2], ys[3])
            share(xs[2], ys[2])
    for copy in siblings:
        copy.wait_recv()
    stay.wait()
    cp.finish()


def gather_keys(own):
    anywhere = pl.BlockSpec(memory_space=pl.ANY)
    return pl.pallas_call(
        keys_kernel,
        out_shape=jax.ShapeDtypeStruct((2, 4, 2, 2, 4, BLOCK, HEAD_SIZE), jnp.bfloat16),
        in_specs=[anywhere],
        out_specs=anywhere,
        scratch_shapes=[
            pltpu.SemaphoreType.DMA((48,)),
            pltpu.SemaphoreType.DMA((48,)),
            pltpu.SemaphoreType.DMA((1,)),
        ],
        compiler_params=pltpu.CompilerParams(collective_id=1, has_side_effects=True),
        name="gather_keys",
    )(own)


def attend_kernel(bounds, q_ref, k_ref, v_ref, first_ref, out_ref):
    block = pl.program_id(0)
    t_low, t_clear, t_edge, t_high, row0 = (bounds[block, i] for i in range(5))
    scale = HEAD_SIZE ** (-0.5) * math.log2(math.e)
    queries = [q_ref[0, :, h * HEAD_SIZE : (h + 1) * HEAD_SIZE] for h in range(2)]

    def tile(masked, t, carry):
        at = pl.ds(pl.multiple_of(t * KEY_TILE, KEY_TILE), KEY_TILE)
        keys, values = k_ref[at, :], v_ref[at, :]
        if masked:
            column = t * KEY_TILE + lax.broadcasted_iota(jnp.int32, (BLOCK, KEY_TILE), 1)
            row = row0 + lax.broadcasted_iota(jnp.int32, (BLOCK, KEY_TILE), 0)
            allowed = (column <= row) & (column >= first_ref[0])
        result = []
        for h in range(2):
            peak, total, summed = carry[3 * h : 3 * h + 3]
            scores = lax.dot_general(
                queries[h], keys, (((1,), (1,)), ((), ())), preferred_element_type=jnp.float32
            )
            if masked:
                scores = jnp.where(allowed, scores, masked_score)
            fresh = jnp.maximum(peak, jnp.max(scores, axis=-1, keepdims=True))
            weights = jnp.exp2((scores - fresh) * scale)
            if masked:
                weights = jnp.where(allowed, weights, 0.0)
            shrink = jnp.exp2((peak - fresh) * scale)
            total = total * shrink + jnp.sum(weights, axis=-1, keepdims=True)
            summed = summed * shrink + jnp.dot(
                weights.astype(jnp.bfloat16), values, preferred_element_type=jnp.float32
            )
            result += [fresh, total, summed]
        return tuple(result)

    carry = (
        jnp.full((BLOCK, 1), masked_score, jnp.float32),
        jnp.zeros((BLOCK, 1), jnp.float32),
        jnp.zeros((BLOCK, HEAD_SIZE), jnp.float32),
    ) * 2
    carry = lax.fori_loop(t_low, t_clear, functools.partial(tile, True), carry)
    carry = lax.fori_loop(t_clear, t_edge, functools.partial(tile, False), carry)
    carry = lax.fori_loop(t_edge, t_high, functools.partial(tile, True), carry)
    for h in range(2):
        out_ref[0, :, h * HEAD_SIZE : (h + 1) * HEAD_SIZE] = (
            carry[3 * h + 2] / carry[3 * h + 1]
        ).astype(jnp.bfloat16)


def attend(bounds, queries, keys, values, first):
    return pl.pallas_call(
        attend_kernel,
        out_shape=jax.ShapeDtypeStruct((4, BLOCK, 2 * HEAD_SIZE), jnp.bfloat16),
        grid_spec=pltpu.PrefetchScalarGridSpec(
            num_scalar_prefetch=1,
            grid=(4,),
            in_specs=[
                pl.BlockSpec((1, BLOCK, 2 * HEAD_SIZE), lambda i, b: (i, 0, 0)),
                pl.BlockSpec((SEQUENCE, HEAD_SIZE), lambda i, b: (0, 0)),
                pl.BlockSpec((SEQUENCE, HEAD_SIZE), lambda i, b: (0, 0)),
                pl.BlockSpec((1, BLOCK, 1), lambda i, b: (i, 0, 0)),
            ],
            out_specs=pl.BlockSpec((1, BLOCK, 2 * HEAD_SIZE), lambda i, b: (i, 0, 0)),
        ),
        compiler_params=pltpu.CompilerParams(vmem_limit_bytes=48 << 20),
        name="attend",
    )(bounds, queries, keys, values, first)


def heads_kernel(own, out, send_sems, recv_sems, local_sem):
    x, y, zh, zl, c = place()
    cz = zh // 2
    partners = [device(x, y, (zh + k) % 4, zl, cc) for k in range(4) for cc in (c, 1 - c)][1:]
    greet(partners)
    spot = lambda j, cc: out.at[:, pl.ds(pl.multiple_of((2 * j + cc) * 256, 256), 256)]
    copies = []
    for k in range(4):
        zt = (zh + k) % 4
        copy = pltpu.make_async_remote_copy(
            src_ref=own.at[zt],
            dst_ref=spot(zh % 2, c),
            send_sem=send_sems.at[k],
            recv_sem=recv_sems.at[(zh % 2) * 2 + c],
            device_id=device(x, y, zt, zl, cz),
            device_id_type=MESH,
        )
        if k == 0:
            stay = pltpu.make_async_copy(own.at[zt], spot(zh % 2, c), local_sem.at[0])
            here = cz == c
            pl.when(here)(stay.start)
            pl.when(jnp.logical_not(here))(copy.start)
        else:
            copy.start()
        copies.append(copy)
    for j in range(2):
        for cc in range(2):
            arrives = pltpu.make_async_remote_copy(
                src_ref=own.at[0],
                dst_ref=spot(j, cc),
                send_sem=send_sems.at[0],
                recv_sem=recv_sems.at[2 * j + cc],
                device_id=partners[0],
                device_id_type=MESH,
            )
            mine = (zh == 2 * c + j) & (c == cc)
            pl.when(jnp.logical_not(mine))(arrives.wait_recv)
    pl.when(here)(stay.wait)
    pl.when(jnp.logical_not(here))(copies[0].wait_send)
    for copy in copies[1:]:
        copy.wait_send()


def exchange_heads(own):
    anywhere = pl.BlockSpec(memory_space=pl.ANY)
    return pl.pallas_call(
        heads_kernel,
        out_shape=jax.ShapeDtypeStruct((BLOCK, 1024), jnp.bfloat16),
        in_specs=[anywhere],
        out_specs=anywhere,
        scratch_shapes=[
            pltpu.SemaphoreType.DMA((4,)),
            pltpu.SemaphoreType.DMA((4,)),
            pltpu.SemaphoreType.DMA((1,)),
        ],
        compiler_params=pltpu.CompilerParams(collective_id=2, has_side_effects=True),
        name="exchange_heads",
    )(own)


def reduce_kernel(partial, hidden, out, landed, joined, arrived, send_sems, recv_sems):
    x, y, zh, zl, c = place()
    sibling, across = device(x, y, zh, zl, 1 - c), device(x, y, zh, 1 - zl, c)
    greet([sibling, across])
    cp = Copies(send_sems, recv_sems)
    pieces = 4
    width = 4096 // pieces
    cut = lambda i: pl.ds(i * width, width)
    first = [
        cp.send(partial.at[1 - zl, 1 - c, :, cut(i)], landed.at[1 - zl, :, cut(i)], sibling)
        for i in range(pieces)
    ]
    second = [
        cp.send(partial.at[zl, 1 - c, :, cut(i)], landed.at[zl, :, cut(i)], sibling)
        for i in range(pieces)
    ]
    third = []
    for i in range(pieces):
        first[i].wait_recv()
        joined[:, cut(i)] = (
            partial[1 - zl, c, :, cut(i)].astype(jnp.float32)
            + landed[1 - zl, :, cut(i)].astype(jnp.float32)
        ).astype(jnp.bfloat16)
        third.append(cp.send(joined.at[:, cut(i)], arrived.at[:, cut(i)], across))
    for i in range(pieces):
        second[i].wait_recv()
        total = partial[zl, c, :, cut(i)].astype(jnp.float32) + landed[zl, :, cut(i)].astype(
            jnp.float32
        )
        third[i].wait_recv()
        total = total + arrived[:, cut(i)].astype(jnp.float32)
        out[:, cut(i)] = (hidden[:, cut(i)].astype(jnp.float32) + total).astype(jnp.bfloat16)
    cp.finish()


def reduce_rows(partial, hidden):
    inside = pl.BlockSpec(memory_space=pltpu.VMEM)
    return pl.pallas_call(
        reduce_kernel,
        out_shape=jax.ShapeDtypeStruct((48, 4096), jnp.bfloat16),
        in_specs=[inside] * 2,
        out_specs=inside,
        scratch_shapes=[
            pltpu.VMEM((2, 48, 4096), jnp.bfloat16),
            pltpu.VMEM((48, 4096), jnp.bfloat16),
            pltpu.VMEM((48, 4096), jnp.bfloat16),
            pltpu.SemaphoreType.DMA((12,)),
            pltpu.SemaphoreType.DMA((12,)),
        ],
        compiler_params=pltpu.CompilerParams(collective_id=3, has_side_effects=True),
        name="reduce_rows",
    )(partial, hidden)


def body(hidden_in, norm_gain, w_query, w_key, value_weight, w_out, doc_ids, positions):
    x, y, zh, zl, c = place()
    normed = rms_normed(hidden_in, norm_gain)
    quarter = lambda w: lax.dynamic_slice_in_dim(w, x * 64, 64, 0)
    queries_w, keys_w, values_w = quarter(w_query), quarter(w_key), quarter(value_weight)
    weights = jnp.stack(
        [
            jnp.concatenate(
                [
                    queries_w[:, j * 512 + cc * 256 : j * 512 + cc * 256 + 256],
                    (values_w if cc else keys_w)[:, j * 128 : j * 128 + 128],
                ],
                axis=1,
            )
            for j in range(2)
            for cc in range(2)
        ]
    )
    meta = jnp.stack([doc_ids, positions]).reshape(2, 1, BLOCK)
    meta = jnp.pad(meta, ((0, 0), (0, 0), (0, 64))).reshape(4, 128)
    meta = jnp.pad(meta, ((0, 4), (0, 0)))
    rows, weights, meta = gather(normed.reshape(2, 24, 4096), weights, meta)
    rows, weights = rows.reshape(768, 4096), weights.reshape(4096, 384)
    meta = jnp.transpose(meta, (0, 2, 1, 3, 4))[:, :, :, :4].reshape(4, 4, 4, 2, 256)[..., :BLOCK]
    documents = meta[..., 0, :].reshape(SEQUENCE)
    mine = lax.dynamic_slice(meta, (x, 0, y, 0, 0), (1, 4, 1, 2, BLOCK)).reshape(4, 2, BLOCK)
    my_documents, my_positions = mine[:, 0], mine[:, 1].reshape(768)
    first = jnp.zeros((4, BLOCK), jnp.int32)
    for d in range(6):
        before = jnp.sum((documents < d).astype(jnp.int32))
        first = jnp.where(my_documents == d, before, first)
    row0 = (x * 16 + jnp.arange(4, dtype=jnp.int32) * 4 + y) * BLOCK
    t_low = first[:, 0] // KEY_TILE
    t_edge = jnp.maximum((row0 + 1) // KEY_TILE, t_low)
    t_clear = jnp.clip((first[:, -1] + KEY_TILE - 1) // KEY_TILE, t_low, t_edge)
    t_high = (row0 + BLOCK - 1) // KEY_TILE + 1
    bounds = jnp.stack([t_low, t_clear, t_edge, t_high, row0], axis=1)

    product = jnp.dot(rows, weights, preferred_element_type=jnp.float32)
    cosine_table, sine_table = yarn_tables(my_positions, HEAD_SIZE)
    turned = apply_rotation(product.reshape(768, 3, HEAD_SIZE), cosine_table, sine_table)
    queries = turned[:, :2].astype(jnp.bfloat16).reshape(4, BLOCK, 2 * HEAD_SIZE)
    own = jnp.where(c == 0, turned[:, 2], product[:, 2 * HEAD_SIZE :]).astype(jnp.bfloat16)
    both = gather_keys(own.reshape(2, 2, BLOCK, HEAD_SIZE))
    both = both.reshape(2, SEQUENCE, HEAD_SIZE)
    attended = attend(bounds, queries, both[0], both[1], first.reshape(4, BLOCK, 1))
    attended = exchange_heads(attended)
    partial = jnp.dot(attended, w_out, preferred_element_type=jnp.float32).astype(jnp.bfloat16)
    return reduce_rows(partial.reshape(2, 2, 48, 4096), hidden_in)


def solution(mesh):
    in_specs = (
        P(("outer", "inner", "tensor"), None),
        P(),
        P("inner", "tensor"),
        P("inner", "tensor"),
        P("inner", "tensor"),
        P("tensor", None),
        P(("outer", "inner")),
        P(("outer", "inner")),
    )
    out_specs = P(("outer", "inner", "tensor"), None)
    return jax.shard_map(body, mesh=mesh, in_specs=in_specs, out_specs=out_specs, check_vma=False)
```

time: 830 us -> 201 us (0.24)
  the two profiles are of different devices: /device:TPU:46 before, /device:TPU:13 now
where the time goes in v1:
time: 201 us; the launch traced here: 200 us
  Pallas kernels  155 us (77%)
  local copies, waits for them, and re-layouts  16.6 us (8%)
  other arithmetic  14.8 us (7%)
  matrix products  13 us (6%)
    pallas_call x1, Pallas kernels, gather(): pl.pallas_call(gather_kernel, out_shape=(jax.ShapeDtypeStruct((8, 2, 2, 2...  51 us
    pallas_call x1, Pallas kernels, attend(): pl.pallas_call(attend_kernel, out_shape=jax.ShapeDtypeStruct((4, BLOCK, 2...  43.8 us
    pallas_call x1, Pallas kernels, gather_keys(): pl.pallas_call(keys_kernel, out_shape=jax.ShapeDtypeStruct((2, 4, 2, 2, 4...  31.2 us
    pallas_call x1, Pallas kernels, reduce_rows(): pl.pallas_call(reduce_kernel, out_shape=jax.ShapeDtypeStruct((48, 4096),...  16.9 us
    pallas_call x1, Pallas kernels, exchange_heads(): pl.pallas_call(heads_kernel, out_shape=jax.ShapeDtypeStruct((BLOCK, 1024)...  12.7 us
    dot_general x1, matrix products, body(): product = jnp.dot(rows, weights, preferred_element_type=jnp.float32)  6.55 us
    dot_general x1, matrix products, body(): jnp.dot(attended, w_out, preferred_element_type=jnp.float32)  6.49 us
    unnamed x12, local copies, waits for them, and re-layouts  5.93 us

profile of v1, /device:TPU:13, one launch (start us, length us, event | category | flops | bytes accessed | tf_op | source)
XLA Modules:
  0.0 200.2 jit_solution(16603475004773288007)
XLA Ops:
  0.0 1.2 fusion
  1.2 1.9 fusion.2
  3.1 0.8 constant_dynamic-slice_fusion
  3.9 0.8 constant_dynamic-slice_fusion.1
  4.8 0.7 pad_maximum_fusion.1.weights
  5.5 0.7 add_bitcast_fusion
  6.2 0.6 pad.9.meta
  6.8 51.0 %gather.1 = (bf16[8,2,2,24,4096]{4,3,2,1,0:T(8,128)(2,1)}, bf16[4,4,4,64,384]{4,3,2,1,0:T(8,128)(2,1)}, s32[4,4,4,8,128]{4,3,2,1,0:T(8,128)}) custom-call(bf16[2,24,4096]{2,1,0:T(8,128)(2,1)} %bitcast.45, bf16[4,64,384]{2,1,0:T(8,128)(2,1)} %pad_maximum_fusion.1.weights, s32[8,128]{1,0:T(8,128)} %pad.9.meta), custom_call_target="tpu_custom_call" | custom-call | tf_op jit(solution)/shard_map/gather/pallas_call | solution.py:251
  57.8 1.0 slice.92
  58.7 0.1 reshape.333
  58.9 1.2 fusion.12
  60.1 3.9 %slice_convert_fusion = (f32[4,1,192]{2,0,1:T(4,128)S(1)}, s32[4,1,192]{2,0,1:T(4,128)S(1)}) fusion(s32[4,2,192]{2,0,1:T(4,128)S(1)} %bitcast.52, s32[]{:T(128)} %get-tuple-element.15, s32[]{:T(128)} %get-tuple-element.14, s32[]{:T(128)} %get-tuple-element.11, s32[]{:T(128)} %get-tuple-element.13, s32[]{:T(128)} %get-tuple-element.12, s32[]{:T(128)} %get-tuple-element.16), kind=kLoop, calls=%fused_computation.38 | loop fusion | flops 9984 | bytes 12312 | tf_op jit(solution)/shard_map/convert_element_type | solution.py:51
  64.0 0.1 fusion.20
  64.1 0.1 stack.40.bounds
  64.2 6.6 %fusion.29 = f32[768,384]{1,0:T(8,128)S(1)} fusion(bf16[768,4096]{1,0:T(8,128)(2,1)} %bitcast.55, bf16[4096,384]{1,0:T(8,128)(2,1)} %bitcast.56), kind=kOutput, calls=%fused_computation.82 | convolution fusion | flops 2415919104 | bytes 10616832 | tf_op jit(solution)/shard_map/dot_general | solution.py:598
  70.8 0.0 copy-start.2
  70.8 0.4 copy.13
  71.2 0.6 copy-done.2
  71.8 0.0 copy-start.3
  71.8 0.1 fusion.28
  71.9 0.4 copy.20
  72.3 1.4 copy.21
  73.7 0.1 convert_element_type.56
  73.8 0.0 copy-done.3
  73.8 1.5 fusion.5
  75.2 1.6 multiply_add_fusion
  76.8 0.2 fusion.4
  77.0 0.4 copy.16
  77.5 0.3 reshape.338.q_ref
  77.7 1.8 fusion.7
  79.5 31.2 %gather_keys.1 = bf16[2,4,2,2,4,192,128]{6,5,4,3,2,1,0:T(8,128)(2,1)} custom-call(bf16[2,2,192,128]{3,2,1,0:T(8,128)(2,1)} %bitcast.46), custom_call_target="tpu_custom_call" | custom-call | tf_op jit(solution)/shard_map/gather_keys/pallas_call | solution.py:364
  110.7 5.2 %fusion.27 = (bf16[1,4,2,2,4,192,128]{6,5,4,3,2,1,0:T(8,128)(2,1)}, bf16[1,4,2,2,4,192,128]{6,5,4,3,2,1,0:T(8,128)(2,1)S(1)}) fusion(bf16[2,4,2,2,4,192,128]{6,5,4,3,2,1,0:T(8,128)(2,1)} %gather_keys.1), kind=kLoop, calls=%fused_computation.80 | loop fusion | bytes 12582912 | tf_op jit(solution)/shard_map/slice | solution.py:605
  115.9 0.9 copy.17.first_ref
  116.8 0.0 copy-start
  116.8 1.0 copy-done
  117.8 43.8 %attend.1.own = bf16[4,192,256]{2,1,0:T(8,128)(2,1)S(1)} custom-call(s32[4,5]{1,0:T(4,128)S(1)} %stack.40.bounds, bf16[4,192,256]{2,1,0:T(8,128)(2,1)S(1)} %reshape.338.q_ref, bf16[12288,128]{1,0:T(8,128)(2,1)S(1)} %bitcast.41, bf16[12288,128]{1,0:T(8,128)(2,1)} %bitcast.42, s32[4,192,1]{2,1,0:T(8,128)S(1)} %copy-done), custom_call_target="tpu_custom_call" | custom-call | tf_op jit(solution)/shard_map/attend/pallas_call | solution.py:427
  161.6 0.0 copy-start.1
  161.6 0.7 copy-done.1
  162.4 12.7 %exchange_heads.1 = bf16[192,1024]{1,0:T(8,128)(2,1)} custom-call(bf16[4,192,256]{2,1,0:T(8,128)(2,1)} %copy-done.1), custom_call_target="tpu_custom_call" | custom-call | tf_op jit(solution)/shard_map/exchange_heads/pallas_call | solution.py:491
  175.1 6.5 %convolution_convert_fusion = bf16[192,4096]{1,0:T(8,128)(2,1)} fusion(bf16[192,1024]{1,0:T(8,128)(2,1)} %exchange_heads.1, bf16[1024,4096]{1,0:T(8,128)(2,1)} %param.14), kind=kOutput, calls=%fused_computation | convolution fusion | flops 1611399168 | bytes 10354688 | tf_op jit(solution)/shard_map/dot_general | solution.py:607
  181.6 16.9 %reduce_rows.1 = bf16[48,4096]{1,0:T(8,128)(2,1)} custom-call(bf16[2,2,48,4096]{3,2,1,0:T(8,128)(2,1)} %bitcast.44, bf16[48,4096]{1,0:T(8,128)(2,1)} %hidden.1), custom_call_target="tpu_custom_call" | custom-call | tf_op jit(solution)/shard_map/reduce_rows/pallas_call | solution.py:543
  198.4 1.8 copy.25
  (11 shorter events, 0.1 us)
Async XLA Ops:
  70.8 1.0 copy-start.2
  71.8 2.0 copy-start.3
  116.8 1.0 copy-start
  161.6 0.7 copy-start.1

commit v2 on v1

v2 whole, which is shorter than its diff:
```python
import functools
import math

import jax
import jax.numpy as jnp
from jax import lax
from jax.experimental import pallas as pl
from jax.experimental.pallas import tpu as pltpu
from jax.sharding import PartitionSpec as P

HEAD_SIZE = 128
BLOCK = 192
SEQUENCE = 12288
KEY_TILE = 1024
KEY_PIECE = 256
MESH = pl.DeviceIdType.MESH


rope_base = 500000.0
yarn_factor = 8.0
trained_context = 8192.0
beta_fast = 32.0
beta_slow = 1.0
norm_epsilon = 1e-05
masked_score = -1e30


def yarn_inverse(head_dim):
    half_dim = head_dim // 2

    def correction(rotations):
        return (
            head_dim
            * math.log(trained_context / (rotations * 2.0 * math.pi))
            / (2.0 * math.log(rope_base))
        )

    lowest = max(math.floor(correction(beta_fast)), 0)
    highest = min(math.ceil(correction(beta_slow)), head_dim - 1)
    spread = max(highest - lowest, 0.001)
    values = []
    for column in range(half_dim):
        extrapolated = rope_base ** (-2.0 * column / head_dim)
        ramp = min(max((column - lowest) / spread, 0.0), 1.0)
        values.append(extrapolated / yarn_factor * ramp + extrapolated * (1.0 - ramp))
    return values


def place():
    outer, inner, tensor = (lax.axis_index(name) for name in ("outer", "inner", "tensor"))
    return outer, inner % 4, inner // 4, tensor // 2, tensor % 2


def device(x, y, zh, zl, c):
    return (x, zh * 4 + y, zl * 2 + c)


def greet(partners):
    barrier = pltpu.get_barrier_semaphore()
    for partner in partners:
        pl.semaphore_signal(barrier, inc=1, device_id=partner, device_id_type=MESH)
    pl.semaphore_wait(barrier, len(partners))


class Copies:
    def __init__(self, send_sems, recv_sems):
        self.send_sems, self.recv_sems, self.count, self.sent = send_sems, recv_sems, 0, []

    def send(self, src, dst, target):
        copy = pltpu.make_async_remote_copy(
            src_ref=src,
            dst_ref=dst,
            send_sem=self.send_sems.at[self.count],
            recv_sem=self.recv_sems.at[self.count],
            device_id=target,
            device_id_type=MESH,
        )
        self.count += 1
        copy.start()
        self.sent.append(copy)
        return copy

    def finish(self):
        for copy in self.sent:
            copy.wait_send()


def front_kernel(
    hidden, gain, w_query, w_key, w_value, doc_ids, positions, inverse,
    q_out, both, first_out,
    rows, weights, meta, meta_own, tables, product, kv, q_sum,
    send_sems, recv_sems, a2a_send, a2a_recv, local_sems,
):
    x, y, zh, zl, c = place()
    p = zh * 2 + zl
    near = lambda q: device(x, y, (q % 8) // 2, q % 2, c)
    right, left = near(p + 1), near(p + 7)
    sibling = device(x, y, zh, zl, 1 - c)
    xs = [(x + k) % 4 for k in range(4)]
    ys = [(y + k) % 4 for k in range(4)]
    y_next, y_far, y_prev = (device(x, ys[k], zh, zl, c) for k in (1, 2, 3))
    x_next, x_far, x_prev = (device(xs[k], y, zh, zl, c) for k in (1, 2, 3))
    columns = [device(x, y, (zh + k) % 4, zl, cc) for k in range(4) for cc in (c, 1 - c)][1:]
    partners = columns + [right, left, y_next, y_prev, y_far, x_next, x_prev, x_far]
    barrier = pltpu.get_barrier_semaphore()
    for partner in partners:
        pl.semaphore_signal(barrier, inc=1, device_id=partner, device_id_type=MESH)
    cp = Copies(send_sems, recv_sems)

    meta_own[...] = jnp.full((8, 128), 99, jnp.int32)
    meta_own[0:1, :] = doc_ids[:, :128]
    meta_own[1:2, :64] = doc_ids[:, 128:]
    meta_own[2:3, :] = positions[:, :128]
    meta_own[3:4, :64] = positions[:, 128:]
    meta[x, y, zh] = meta_own[...]
    widened = hidden[...].astype(jnp.float32)
    power = jnp.mean(widened * widened, axis=-1, keepdims=True)
    rows[p, c] = (widened * lax.rsqrt(power + norm_epsilon) * gain[...]).astype(jnp.bfloat16)
    pl.semaphore_wait(barrier, len(partners))

    a2a = []
    landing = (pl.ds(0, 256), pl.ds(256, 128))
    for j in range(2):
        for cc in range(2):
            zt = 2 * c + j
            own = (zt == zh) & (c == cc)
            taken = pl.ds(pl.multiple_of(x * 64, 64), 64)
            sources = (
                w_query.at[taken, pl.ds(j * 512 + cc * 256, 256)],
                (w_value if cc else w_key).at[taken, pl.ds(j * 128, 128)],
            )
            for i in range(2):
                spot = weights.at[zh, y, x, :, landing[i]]
                copy = pltpu.make_async_remote_copy(
                    src_ref=sources[i],
                    dst_ref=spot,
                    send_sem=a2a_send.at[4 * j + 2 * cc + i],
                    recv_sem=a2a_recv.at[2 * zh + i],
                    device_id=device(x, y, zt, zl, cc),
                    device_id_type=MESH,
                )
                stay = pltpu.make_async_copy(sources[i], spot, local_sems.at[i])
                pl.when(own)(stay.start)
                pl.when(jnp.logical_not(own))(copy.start)
                a2a.append((own, copy, stay))
    chunks_right = (pl.ds(0, 16), pl.ds(16, 32))
    chunks_left = (pl.ds(32, 16), pl.ds(0, 32))
    to_right, to_left, to_sibling = {}, {}, []
    same = lambda ref, target: cp.send(ref, ref, target)
    meta_z = [
        cp.send(meta_own, meta.at[x, y, zh], device(x, y, (zh + k) % 4, zl, c)) for k in (1, 2, 3)
    ]
    for h in range(2):
        to_right[0, h] = same(rows.at[p, c, chunks_right[h]], right)
        to_left[0, h] = same(rows.at[p, c, chunks_left[h]], left)
    to_sibling.append(same(rows.at[p, c], sibling))

    for source in range(4):
        for i in range(2):
            arrives = pltpu.make_async_remote_copy(
                src_ref=weights.at[source, y, x, :, landing[i]],
                dst_ref=weights.at[source, y, x, :, landing[i]],
                send_sem=a2a_send.at[0],
                recv_sem=a2a_recv.at[2 * source + i],
                device_id=sibling,
                device_id_type=MESH,
            )
            own = (zh == source) & (c == zh // 2)
            pl.when(jnp.logical_not(own))(arrives.wait_recv)
    for own, copy, stay in a2a:
        pl.when(own)(stay.wait)
    mine = weights.at[:, y, x]
    wy_next, wy_prev = same(mine, y_next), same(mine, y_prev)
    wx, forwards = {}, []

    def along_x(k):
        piece = weights.at[:, ys[k], x]
        wx[len(wx)] = (ys[k], same(piece, x_next), same(piece, x_prev))

    def forward_x(k):
        yy, a, b = wx[k]
        a.wait_recv()
        forwards.append(same(weights.at[pl.ds(0, 2), yy, xs[3]], x_next))
        b.wait_recv()
        forwards.append(same(weights.at[pl.ds(2, 2), yy, xs[1]], x_prev))

    def ring(step):
        for h in range(2):
            for to, chunks, target, hop in (
                (to_right, chunks_right, right, 7),
                (to_left, chunks_left, left, 1),
            ):
                to[step, h].wait_recv()
                q = (p + hop * (step + 1)) % 8
                if step < 3:
                    spot = rows.at[q, c, chunks[h]]
                    to_sibling.append(same(spot, sibling))
                    if step < 2:
                        to[step + 1, h] = same(spot, target)
                    else:
                        to[3, h] = same(far_spot(q, h, hop), target)
                else:
                    to_sibling.append(same(far_spot(q, h, hop), sibling))

    def far_spot(q, h, hop):
        if h == 0:
            return rows.at[q, c, pl.ds(0, 16) if hop == 7 else pl.ds(32, 16)]
        return rows.at[q, c, pl.ds(16, 16), pl.ds(0 if hop == 7 else 2048, 2048)]

    along_x(0)
    for copy in meta_z:
        copy.wait_recv()
    mine = meta.at[x, y]
    meta_y = [same(mine, target) for target in (y_next, y_far, y_prev)]
    ring(0)
    wy_next.wait_recv()
    wy_far_next = same(weights.at[pl.ds(0, 2), ys[3], x], y_next)
    along_x(3)
    wy_prev.wait_recv()
    wy_far_prev = same(weights.at[pl.ds(2, 2), ys[1], x], y_prev)
    along_x(1)
    for copy in meta_y:
        copy.wait_recv()
    mine = meta.at[x]
    meta_x = [same(mine, target) for target in (x_next, x_far, x_prev)]
    forward_x(0)
    wy_far_next.wait_recv()
    wy_far_prev.wait_recv()
    along_x(2)

    def tables_of(zb):
        tile = meta[x, y, zb].astype(jnp.float32)
        upper = jnp.broadcast_to(tile[2:3], (128, 128)).T
        lower = jnp.broadcast_to(tile[3:4], (128, 128)).T
        angles = jnp.concatenate([upper, lower[:64]], axis=0) * inverse[...]
        attention_gain = 0.1 * math.log(yarn_factor) + 1.0
        lane = lax.broadcasted_iota(jnp.int32, (BLOCK, HEAD_SIZE), 1)
        sine = jnp.sin(angles) * attention_gain
        tables[0, zb] = jnp.cos(angles) * attention_gain
        tables[1, zb] = jnp.where(lane < HEAD_SIZE // 2, -sine, sine)

    tables_of(0)
    tables_of(1)
    ring(1)
    tables_of(2)
    forward_x(1)
    forward_x(2)
    tables_of(3)
    ring(2)
    forward_x(3)
    for copy in meta_x:
        copy.wait_recv()
    everything = meta[...].reshape(64, 8, 128)
    line = lax.broadcasted_iota(jnp.int32, (8, 128), 0)
    firsts = []
    for d in range(1, 6):
        hits = jnp.sum(jnp.where(everything < d, 1, 0), axis=0)
        hits = jnp.where(line < 2, hits, 0).astype(jnp.float32)
        firsts.append(jnp.sum(jnp.sum(hits, axis=0, keepdims=True), axis=1, keepdims=True))
    for zb in range(4):
        documents = meta[x, y, zb][0:2]
        first = jnp.zeros((2, 128), jnp.float32)
        for d in range(1, 6):
            first = jnp.where(documents == d, firsts[d - 1], first)
        first_out[2 * zb : 2 * zb + 2, :] = first.astype(jnp.int32)
    ring(3)
    for copy in forwards + to_sibling:
        copy.wait_recv()

    def depth(k):
        return pl.ds(pl.multiple_of(k * 256, 256), 256)

    product[...] = jnp.zeros_like(product)

    @pl.loop(0, 16)
    def _(k):
        piece = weights[k // 4, k % 4, :, :, 256:384].reshape(256, HEAD_SIZE)
        left_side = rows[:, :, :, depth(k)].reshape(768, 256)
        product[...] += jnp.dot(left_side, piece, preferred_element_type=jnp.float32)

    def turn(head, cosine, sine):
        return head * cosine + pltpu.roll(head, HEAD_SIZE // 2, 1) * sine

    is_key = c == 0
    for zb in range(4):
        head = product[zb * BLOCK : (zb + 1) * BLOCK, :]
        cosine = jnp.where(is_key, tables[0, zb], 1.0)
        sine = jnp.where(is_key, tables[1, zb], 0.0)
        kv[zb // 2, zb % 2] = turn(head, cosine, sine).astype(jnp.bfloat16)

    whole = lambda xx, yy: both.at[c, xx, :, :, yy]
    half = lambda f, xx, yy: both.at[c, xx, f, :, yy]
    part = lambda a, xx, yy: both.at[c, xx, :, a, yy]
    cell = lambda f, a, xx, yy: both.at[c, xx, f, a, yy]
    from_y_prev = cp.send(kv, whole(x, y), y_next)
    from_x_prev = cp.send(kv, whole(x, y), x_next)
    from_y_next = cp.send(kv, whole(x, y), y_prev)
    from_x_next = cp.send(kv, whole(x, y), x_prev)
    siblings = [cp.send(kv, whole(x, y), sibling)]
    stay = pltpu.make_async_copy(kv, whole(x, y), local_sems.at[2])
    stay.start()

    def queries_of(zb):
        q_sum[...] = jnp.zeros_like(q_sum)

        @pl.loop(0, 16)
        def _(k):
            piece = weights[k // 4, k % 4, :, :, 0:256].reshape(256, 256)
            left_side = rows[2 * zb : 2 * zb + 2, :, :, depth(k)].reshape(BLOCK, 256)
            q_sum[...] += jnp.dot(left_side, piece, preferred_element_type=jnp.float32)

        for h in range(2):
            at = pl.ds(h * HEAD_SIZE, HEAD_SIZE)
            q_out[zb, :, at] = turn(q_sum[:, at], tables[0, zb], tables[1, zb]).astype(jnp.bfloat16)

    def share(xx, yy):
        siblings.append(same(whole(xx, yy), sibling))

    a_prev, a_next, b_prev, b_next = {}, {}, {}, {}

    def a_send(k):
        a_prev[k] = same(part(0, x, ys[k]), x_next)
        a_next[k] = same(part(0, x, ys[k]), x_prev)

    def b_send(k):
        b_prev[k] = same(part(1, xs[k], y), y_next)
        b_next[k] = same(part(1, xs[k], y), y_prev)

    queries_of(0)
    queries_of(1)
    from_y_prev.wait_recv()
    y_far_prev = same(half(0, x, ys[3]), y_next)
    a_send(3)
    from_x_prev.wait_recv()
    x_far_prev = same(half(0, xs[3], y), x_next)
    b_send(3)
    from_y_next.wait_recv()
    y_far_next = same(half(1, x, ys[1]), y_prev)
    a_send(1)
    from_x_next.wait_recv()
    x_far_next = same(half(1, xs[1], y), x_prev)
    b_send(1)
    for xx, yy in ((0, 3), (0, 1), (3, 0), (1, 0)):
        share(xs[xx], ys[yy])
    queries_of(2)
    y_far_prev.wait_recv()
    y_far_next.wait_recv()
    a_send(2)
    x_far_prev.wait_recv()
    x_far_next.wait_recv()
    b_send(2)
    share(x, ys[2])
    share(xs[2], y)
    fa, fb = {}, {}
    for k in (3, 1, 2):
        a_prev[k].wait_recv()
        fa[k, 0] = same(cell(0, 0, xs[3], ys[k]), x_next)
        b_prev[k].wait_recv()
        fb[k, 0] = same(cell(0, 1, xs[k], ys[3]), y_next)
        a_next[k].wait_recv()
        fa[k, 1] = same(cell(1, 0, xs[1], ys[k]), x_prev)
        b_next[k].wait_recv()
        fb[k, 1] = same(cell(1, 1, xs[k], ys[1]), y_prev)
        if k == 1:
            for xx in (1, 3):
                for yy in (1, 3):
                    share(xs[xx], ys[yy])
            queries_of(3)
    for k in (3, 1, 2):
        for f in range(2):
            fa[k, f].wait_recv()
            fb[k, f].wait_recv()
    for xx, yy in ((1, 2), (3, 2), (2, 1), (2, 3), (2, 2)):
        share(xs[xx], ys[yy])
    for copy in siblings:
        copy.wait_recv()
    stay.wait()
    for own, copy, _ in a2a:
        pl.when(jnp.logical_not(own))(copy.wait_send)
    cp.finish()


def front(hidden, gain, w_query, w_key, w_value, doc_ids, positions, inverse):
    anywhere = pl.BlockSpec(memory_space=pl.ANY)
    inside = pl.BlockSpec(memory_space=pltpu.VMEM)
    return pl.pallas_call(
        front_kernel,
        out_shape=(
            jax.ShapeDtypeStruct((4, BLOCK, 2 * HEAD_SIZE), jnp.bfloat16),
            jax.ShapeDtypeStruct((2, 4, 2, 2, 4, BLOCK, HEAD_SIZE), jnp.bfloat16),
            jax.ShapeDtypeStruct((8, 128), jnp.int32),
        ),
        in_specs=[inside, inside, anywhere, anywhere, anywhere, inside, inside, inside],
        out_specs=(inside, anywhere, inside),
        scratch_shapes=[
            pltpu.VMEM((8, 2, 48, 4096), jnp.bfloat16),
            pltpu.VMEM((4, 4, 4, 64, 384), jnp.bfloat16),
            pltpu.VMEM((4, 4, 4, 8, 128), jnp.int32),
            pltpu.VMEM((8, 128), jnp.int32),
            pltpu.VMEM((2, 4, BLOCK, HEAD_SIZE), jnp.float32),
            pltpu.VMEM((768, HEAD_SIZE), jnp.float32),
            pltpu.VMEM((2, 2, BLOCK, HEAD_SIZE), jnp.bfloat16),
            pltpu.VMEM((BLOCK, 2 * HEAD_SIZE), jnp.float32),
            pltpu.SemaphoreType.DMA((120,)),
            pltpu.SemaphoreType.DMA((120,)),
            pltpu.SemaphoreType.DMA((8,)),
            pltpu.SemaphoreType.DMA((8,)),
            pltpu.SemaphoreType.DMA((3,)),
        ],
        compiler_params=pltpu.CompilerParams(
            collective_id=0, has_side_effects=True, vmem_limit_bytes=32 << 20
        ),
        name="front",
    )(hidden, gain, w_query, w_key, w_value, doc_ids, positions, inverse)


def attend_kernel(bounds, q_ref, k_ref, v_ref, first_ref, out_ref, even, odd, summed):
    block = pl.program_id(0)
    t_low, t_clear, t_edge, t_high, row0 = (bounds[block, i] for i in range(5))
    scale = HEAD_SIZE ** (-0.5) * math.log2(math.e)
    width = 2 * BLOCK
    queries = jnp.concatenate([q_ref[0, :, :HEAD_SIZE], q_ref[0, :, HEAD_SIZE:]], axis=0)
    summed[...] = jnp.zeros_like(summed)

    half = KEY_TILE // 2

    def produce(store, begin, masked):
        peak = None
        for u in range(half // KEY_PIECE):
            first_key = begin + u * KEY_PIECE
            keys = k_ref[pl.ds(pl.multiple_of(first_key, KEY_PIECE), KEY_PIECE), :]
            piece = lax.dot_general(
                keys, queries, (((1,), (1,)), ((), ())), preferred_element_type=jnp.float32
            )
            if masked:
                key = first_key + lax.broadcasted_iota(jnp.int32, (KEY_PIECE, width), 0)
                lane = lax.broadcasted_iota(jnp.int32, (1, width), 1)
                query = row0 + jnp.where(lane < BLOCK, lane, lane - BLOCK)
                allowed = (key <= query) & (key >= first_ref[0])
                piece = jnp.where(allowed, piece, masked_score)
            store[u * KEY_PIECE : (u + 1) * KEY_PIECE, :] = piece
            top = jnp.max(piece.reshape(KEY_PIECE // 8, 8, width), axis=0)
            peak = top if peak is None else jnp.maximum(peak, top)
        return peak

    def consume(store, begin, peak, total, fresh):
        latest = jnp.maximum(peak, jnp.max(fresh, axis=0, keepdims=True))
        shrink = jnp.exp2((peak - latest) * scale)
        total = total * shrink
        offset = latest * scale
        gained = None
        for u in range(half // KEY_PIECE):
            weights = jnp.exp2(store[u * KEY_PIECE : (u + 1) * KEY_PIECE, :] * scale - offset)
            total = total + jnp.sum(weights.reshape(KEY_PIECE // 8, 8, width), axis=0)
            values = v_ref[pl.ds(pl.multiple_of(begin + u * KEY_PIECE, KEY_PIECE), KEY_PIECE), :]
            term = lax.dot_general(
                values, weights.astype(jnp.bfloat16), (((0,), (0,)), ((), ())),
                preferred_element_type=jnp.float32,
            )
            gained = term if gained is None else gained + term
        summed[...] = summed[...] * shrink + gained
        return latest, total

    def step(masked, t, carry):
        peak, total, fresh = carry
        begin = t * KEY_TILE
        following = produce(even, begin, masked)
        peak, total = consume(odd, begin - half, peak, total, fresh)
        fresh = produce(odd, begin + half, masked)
        peak, total = consume(even, begin, peak, total, following)
        return peak, total, fresh

    begin = t_low * KEY_TILE
    peak, total = jnp.full((1, width), masked_score, jnp.float32), jnp.zeros((8, width), jnp.float32)
    following = produce(even, begin, True)
    fresh = produce(odd, begin + half, True)
    peak, total = consume(even, begin, peak, total, following)
    carry = (peak, total, fresh)
    start = t_low + 1
    carry = lax.fori_loop(start, t_clear, functools.partial(step, True), carry)
    carry = lax.fori_loop(jnp.maximum(t_clear, start), t_edge, functools.partial(step, False), carry)
    carry = lax.fori_loop(jnp.maximum(t_edge, start), t_high, functools.partial(step, True), carry)
    peak, total = consume(odd, t_high * KEY_TILE - half, *carry)
    total = jnp.sum(total, axis=0, keepdims=True)
    result = (summed[...] / total).T
    out_ref[0, :, :HEAD_SIZE] = result[:BLOCK].astype(jnp.bfloat16)
    out_ref[0, :, HEAD_SIZE:] = result[BLOCK:].astype(jnp.bfloat16)


def attend(bounds, queries, both, first):
    return pl.pallas_call(
        attend_kernel,
        out_shape=jax.ShapeDtypeStruct((4, BLOCK, 2 * HEAD_SIZE), jnp.bfloat16),
        grid_spec=pltpu.PrefetchScalarGridSpec(
            num_scalar_prefetch=1,
            grid=(4,),
            in_specs=[
                pl.BlockSpec((1, BLOCK, 2 * HEAD_SIZE), lambda i, b: (i, 0, 0)),
                pl.BlockSpec((None, SEQUENCE, HEAD_SIZE), lambda i, b: (0, 0, 0)),
                pl.BlockSpec((None, SEQUENCE, HEAD_SIZE), lambda i, b: (1, 0, 0)),
                pl.BlockSpec((1, 1, 2 * BLOCK), lambda i, b: (i, 0, 0)),
            ],
            out_specs=pl.BlockSpec((1, BLOCK, 2 * HEAD_SIZE), lambda i, b: (i, 0, 0)),
            scratch_shapes=[
                pltpu.VMEM((KEY_TILE // 2, 2 * BLOCK), jnp.float32),
                pltpu.VMEM((KEY_TILE // 2, 2 * BLOCK), jnp.float32),
                pltpu.VMEM((HEAD_SIZE, 2 * BLOCK), jnp.float32),
            ],
        ),
        compiler_params=pltpu.CompilerParams(vmem_limit_bytes=48 << 20),
        name="attend",
    )(bounds, queries, both, both, first)


def back_kernel(
    own, w_out, hidden, out,
    attended, weights, mine, given, landed, joined, arrived,
    send_sems, recv_sems, local_sems, step_send, step_recv,
):
    x, y, zh, zl, c = place()
    cz = zh // 2
    sibling, across = device(x, y, zh, zl, 1 - c), device(x, y, zh, 1 - zl, c)
    partners = [device(x, y, (zh + k) % 4, zl, cc) for k in range(4) for cc in (c, 1 - c)][1:]
    partners.append(across)
    pieces = 4
    width = 4096 // pieces
    cut = lambda i: pl.ds(i * width, width)
    fetch = [
        pltpu.make_async_copy(w_out.at[:, cut(i)], weights.at[:, cut(i)], local_sems.at[1 + i])
        for i in range(pieces)
    ]
    for copy in fetch:
        copy.start()
    greet(partners)
    spot = lambda j, cc: attended.at[:, pl.ds(pl.multiple_of((2 * j + cc) * 256, 256), 256)]
    copies = []
    here = cz == c
    for k in (2, 1, 3, 0):
        zt = (zh + k) % 4
        copy = pltpu.make_async_remote_copy(
            src_ref=own.at[zt],
            dst_ref=spot(zh % 2, c),
            send_sem=send_sems.at[k],
            recv_sem=recv_sems.at[(zh % 2) * 2 + c],
            device_id=device(x, y, zt, zl, cz),
            device_id_type=MESH,
        )
        if k == 0:
            stay = pltpu.make_async_copy(own.at[zt], spot(zh % 2, c), local_sems.at[0])
            pl.when(here)(stay.start)
            pl.when(jnp.logical_not(here))(copy.start)
        else:
            copy.start()
        copies.append(copy)
    for j in range(2):
        for cc in range(2):
            arrives = pltpu.make_async_remote_copy(
                src_ref=own.at[0],
                dst_ref=spot(j, cc),
                send_sem=send_sems.at[0],
                recv_sem=recv_sems.at[2 * j + cc],
                device_id=sibling,
                device_id_type=MESH,
            )
            local = (zh == 2 * c + j) & (c == cc)
            pl.when(jnp.logical_not(local))(arrives.wait_recv)
    pl.when(here)(stay.wait)

    cp = Copies(step_send, step_recv)
    to_sibling, to_across = [], []

    def pass_on(i):
        to_sibling[i].wait_recv()
        joined[i] = (mine[i, 1 - zl] + landed[i, 1 - zl].astype(jnp.float32)).astype(jnp.bfloat16)
        to_across.append(cp.send(joined.at[i], arrived.at[i], across))

    for i in range(pieces):
        fetch[i].wait()
        term = jnp.dot(attended[...], weights[:, cut(i)], preferred_element_type=jnp.float32)
        term = term.reshape(2, 2, 48, width)
        mine[i] = jnp.where(c == 0, term[:, 0], term[:, 1])
        given[i] = jnp.where(c == 0, term[:, 1], term[:, 0]).astype(jnp.bfloat16)
        to_sibling.append(cp.send(given.at[i], landed.at[i], sibling))
        if i > 0:
            pass_on(i - 1)
    pass_on(pieces - 1)
    for i in range(pieces):
        total = mine[i, zl] + landed[i, zl].astype(jnp.float32)
        to_across[i].wait_recv()
        total = total + arrived[i].astype(jnp.float32)
        out[:, cut(i)] = (hidden[:, cut(i)].astype(jnp.float32) + total).astype(jnp.bfloat16)
    pl.when(jnp.logical_not(here))(copies[-1].wait_send)
    for copy in copies[:-1]:
        copy.wait_send()
    cp.finish()


def back(own, w_out, hidden):
    anywhere = pl.BlockSpec(memory_space=pl.ANY)
    inside = pl.BlockSpec(memory_space=pltpu.VMEM)
    return pl.pallas_call(
        back_kernel,
        out_shape=jax.ShapeDtypeStruct((48, 4096), jnp.bfloat16),
        in_specs=[anywhere, anywhere, inside],
        out_specs=inside,
        scratch_shapes=[
            pltpu.VMEM((BLOCK, 1024), jnp.bfloat16),
            pltpu.VMEM((1024, 4096), jnp.bfloat16),
            pltpu.VMEM((4, 2, 48, 1024), jnp.float32),
            pltpu.VMEM((4, 2, 48, 1024), jnp.bfloat16),
            pltpu.VMEM((4, 2, 48, 1024), jnp.bfloat16),
            pltpu.VMEM((4, 48, 1024), jnp.bfloat16),
            pltpu.VMEM((4, 48, 1024), jnp.bfloat16),
            pltpu.SemaphoreType.DMA((4,)),
            pltpu.SemaphoreType.DMA((4,)),
            pltpu.SemaphoreType.DMA((5,)),
            pltpu.SemaphoreType.DMA((8,)),
            pltpu.SemaphoreType.DMA((8,)),
        ],
        compiler_params=pltpu.CompilerParams(
            collective_id=1, has_side_effects=True, vmem_limit_bytes=32 << 20
        ),
        name="back",
    )(own, w_out, hidden)


def body(hidden_in, norm_gain, w_query, w_key, value_weight, w_out, doc_ids, positions):
    x, y, zh, zl, c = place()
    inverse = yarn_inverse(HEAD_SIZE)
    queries, both, first = front(
        hidden_in,
        norm_gain.reshape(1, 4096),
        w_query,
        w_key,
        value_weight,
        doc_ids.reshape(1, BLOCK),
        positions.reshape(1, BLOCK),
        jnp.asarray([inverse + inverse], dtype=jnp.float32),
    )
    first = first.reshape(4, 256)[:, :BLOCK]
    row0 = (x * 16 + jnp.arange(4, dtype=jnp.int32) * 4 + y) * BLOCK
    t_low = first[:, 0] // KEY_TILE
    t_edge = jnp.maximum((row0 + 1) // KEY_TILE, t_low)
    t_clear = jnp.clip((first[:, -1] + KEY_TILE - 1) // KEY_TILE, t_low, t_edge)
    t_high = (row0 + BLOCK - 1) // KEY_TILE + 1
    bounds = jnp.stack([t_low, t_clear, t_edge, t_high, row0], axis=1)
    lanes = jnp.concatenate([first, first], axis=1).reshape(4, 1, 2 * BLOCK)
    attended = attend(bounds, queries, both.reshape(2, SEQUENCE, HEAD_SIZE), lanes)
    return back(attended, w_out, hidden_in)


def solution(mesh):
    in_specs = (
        P(("outer", "inner", "tensor"), None),
        P(),
        P("inner", "tensor"),
        P("inner", "tensor"),
        P("inner", "tensor"),
        P("tensor", None),
        P(("outer", "inner")),
        P(("outer", "inner")),
    )
    out_specs = P(("outer", "inner", "tensor"), None)
    return jax.shard_map(body, mesh=mesh, in_specs=in_specs, out_specs=out_specs, check_vma=False)
```

time: 201 us -> 145 us (0.72)
  the two profiles are of different devices: /device:TPU:13 before, /device:TPU:46 now
where the time goes in v2:
time: 145 us; the launch traced here: 143 us
  Pallas kernels  132 us (91%)
  local copies, waits for them, and re-layouts  10.1 us (7%)
    pallas_call x1, Pallas kernels, front(): pl.pallas_call(front_kernel, out_shape=(jax.ShapeDtypeStruct((4, BLOCK, 2...  79.6 us
    pallas_call x1, Pallas kernels, back(): pl.pallas_call(back_kernel, out_shape=jax.ShapeDtypeStruct((48, 4096), jn...  29.1 us
    pallas_call x1, Pallas kernels, attend(): pl.pallas_call(attend_kernel, out_shape=jax.ShapeDtypeStruct((4, BLOCK, 2...  23.4 us
    unnamed x23, local copies, waits for them, and re-layouts  9.97 us

profile of v2, /device:TPU:46, one launch (start us, length us, event | category | flops | bytes accessed | tf_op | source)
XLA Modules:
  0.0 142.5 jit_solution(13192989144519474857)
XLA Ops:
  0.0 0.0 copy-start.2
  0.0 1.0 copy-done.2
  1.0 0.0 copy-start.4
  1.0 1.0 copy-done.4
  2.0 0.0 copy-start.5
  2.0 0.9 copy-done.5
  3.0 0.0 copy-start.6
  3.0 0.9 copy-done.6
  3.9 0.0 copy-start.7
  3.9 0.7 copy-done.7
  4.6 0.0 copy-start.8
  4.6 0.7 copy-done.8
  5.3 0.0 copy-start.9
  5.3 0.7 copy-done.9
  5.9 0.0 copy-start.10
  5.9 0.7 copy-done.10
  6.6 0.0 copy-start.3
  6.6 79.6 %front.1 = (bf16[4,192,256]{2,1,0:T(8,128)(2,1)S(1)}, bf16[2,4,2,2,4,192,128]{6,5,4,3,2,1,0:T(8,128)(2,1)S(1)}, s32[8,128]{1,0:T(8,128)S(1)}) custom-call(bf16[48,4096]{1,0:T(8,128)(2,1)S(1)} %copy-done.2, f32[1,4096]{1,0:T(1,128)S(1)} %bitcast.7, bf16[256,1024]{1,0:T(8,128)(2,1)S(1)} %copy-done.4, bf16[256,256]{1,0:T(8,128)(2,1)S(1)} %copy-done.5, ...), custom_call_target="tpu_custom_call" | custom-call | tf_op jit(solution)/shard_map/front/pallas_call | solution.py:386
  86.2 0.0 copy-start
  86.2 2.6 %copy-done = bf16[2,4,2,2,4,192,128]{6,5,4,3,2,1,0:T(8,128)(2,1)} copy-done((bf16[2,4,2,2,4,192,128]{6,5,4,3,2,1,0:T(8,128)(2,1)}, bf16[2,4,2,2,4,192,128]{6,5,4,3,2,1,0:T(8,128)(2,1)S(1)}, u32[]{:S(2)}) %copy-start) | copy-done | bytes 6291480
  88.9 0.1 pad_add_fusion
  89.0 0.1 fusion.5
  89.1 0.1 stack.2.bounds
  89.2 0.0 copy-start.1
  89.2 23.4 %attend.1.own = bf16[4,192,256]{2,1,0:T(8,128)(2,1)S(1)} custom-call(s32[4,5]{1,0:T(4,128)S(1)} %stack.2.bounds, bf16[4,192,256]{2,1,0:T(8,128)(2,1)S(1)} %get-tuple-element.9.q_ref, bf16[2,12288,128]{2,1,0:T(8,128)(2,1)} %bitcast.5, bf16[2,12288,128]{2,1,0:T(8,128)(2,1)} %bitcast.6, s32[4,1,384]{2,1,0:T(1,128)S(1)} %reshape.141.first_ref), custom_call_target="tpu_custom_call" | custom-call | tf_op jit(solution)/shard_map/attend/pallas_call | solution.py:491
  112.6 0.0 copy-done.3
  112.6 0.0 copy-done.1
  112.6 29.1 %back.1 = bf16[48,4096]{1,0:T(8,128)(2,1)S(1)} custom-call(bf16[4,192,256]{2,1,0:T(8,128)(2,1)S(1)} %attend.1.own, bf16[1024,4096]{1,0:T(8,128)(2,1)S(1)} %copy-done.1, bf16[48,4096]{1,0:T(8,128)(2,1)S(1)} %copy-done.3), custom_call_target="tpu_custom_call" | custom-call | tf_op jit(solution)/shard_map/back/pallas_call | solution.py:601
  141.8 0.7 copy.11
  (4 shorter events, 0.0 us)
Async XLA Ops:
  0.0 1.0 copy-start.2
  1.0 1.0 copy-start.4
  2.0 0.9 copy-start.5
  3.0 0.9 copy-start.6
  3.9 0.7 copy-start.7
  4.6 0.7 copy-start.8
  5.3 0.7 copy-start.9
  5.9 0.7 copy-start.10
  6.6 106.0 %copy-start.3 = (bf16[48,4096]{1,0:T(8,128)(2,1)S(1)}, bf16[48,4096]{1,0:T(8,128)(2,1)}, u32[]{:S(2)}) copy-start(bf16[48,4096]{1,0:T(8,128)(2,1)} %hidden.3) | copy-start | bytes 1179652
  86.2 2.7 %copy-start = (bf16[2,4,2,2,4,192,128]{6,5,4,3,2,1,0:T(8,128)(2,1)}, bf16[2,4,2,2,4,192,128]{6,5,4,3,2,1,0:T(8,128)(2,1)S(1)}, u32[]{:S(2)}) copy-start(bf16[2,4,2,2,4,192,128]{6,5,4,3,2,1,0:T(8,128)(2,1)S(1)} %get-tuple-element.10) | copy-start | bytes 18874372
  89.2 23.5 %copy-start.1 = (bf16[1024,4096]{1,0:T(8,128)(2,1)S(1)}, bf16[1024,4096]{1,0:T(8,128)(2,1)}, u32[]{:S(2)}) copy-start(bf16[1024,4096]{1,0:T(8,128)(2,1)} %w_out.1) | copy-start | bytes 25165828

commit v3 on v2

--- a/solution.py
+++ b/solution.py
@@ -86,9 +86,9 @@
 
 
 def front_kernel(
-    hidden, gain, w_query, w_key, w_value, doc_ids, positions, inverse,
+    hidden_in, gain_in, w_query, w_key, w_value, doc_ids_in, positions_in, inverse_in,
     q_out, both, first_out,
-    rows, weights, meta, meta_own, tables, product, kv, q_sum,
+    hidden, gain, doc_ids, positions, inverse, rows, weights, meta, meta_own, tables, product, kv, q_sum,
     send_sems, recv_sems, a2a_send, a2a_recv, local_sems,
 ):
     x, y, zh, zl, c = place()
@@ -106,6 +106,22 @@
     for partner in partners:
         pl.semaphore_signal(barrier, inc=1, device_id=partner, device_id_type=MESH)
     cp = Copies(send_sems, recv_sems)
+    fetches = [
+        pltpu.make_async_copy(source, target, local_sems.at[i])
+        for i, (source, target) in enumerate(
+            (
+                (doc_ids_in, doc_ids),
+                (positions_in, positions),
+                (hidden_in, hidden),
+                (gain_in, gain),
+                (inverse_in, inverse),
+            )
+        )
+    ]
+    for copy in fetches:
+        copy.start()
+    fetches[0].wait()
+    fetches[1].wait()
 
     meta_own[...] = jnp.full((8, 128), 99, jnp.int32)
     meta_own[0:1, :] = doc_ids[:, :128]
@@ -113,6 +129,8 @@
     meta_own[2:3, :] = positions[:, :128]
     meta_own[3:4, :64] = positions[:, 128:]
     meta[x, y, zh] = meta_own[...]
+    for copy in fetches[2:]:
+        copy.wait()
     widened = hidden[...].astype(jnp.float32)
     power = jnp.mean(widened * widened, axis=-1, keepdims=True)
     rows[p, c] = (widened * lax.rsqrt(power + norm_epsilon) * gain[...]).astype(jnp.bfloat16)
@@ -381,7 +399,7 @@
 
 
 def front(hidden, gain, w_query, w_key, w_value, doc_ids, positions, inverse):
-    anywhere = pl.BlockSpec(memory_space=pl.ANY)
+    outside = pl.BlockSpec(memory_space=pltpu.HBM)
     inside = pl.BlockSpec(memory_space=pltpu.VMEM)
     return pl.pallas_call(
         front_kernel,
@@ -390,9 +408,14 @@
             jax.ShapeDtypeStruct((2, 4, 2, 2, 4, BLOCK, HEAD_SIZE), jnp.bfloat16),
             jax.ShapeDtypeStruct((8, 128), jnp.int32),
         ),
-        in_specs=[inside, inside, anywhere, anywhere, anywhere, inside, inside, inside],
-        out_specs=(inside, anywhere, inside),
+        in_specs=[outside] * 8,
+        out_specs=(inside, outside, inside),
         scratch_shapes=[
+            pltpu.VMEM((48, 4096), jnp.bfloat16),
+            pltpu.VMEM((1, 4096), jnp.float32),
+            pltpu.VMEM((1, BLOCK), jnp.int32),
+            pltpu.VMEM((1, BLOCK), jnp.int32),
+            pltpu.VMEM((1, HEAD_SIZE), jnp.float32),
             pltpu.VMEM((8, 2, 48, 4096), jnp.bfloat16),
             pltpu.VMEM((4, 4, 4, 64, 384), jnp.bfloat16),
             pltpu.VMEM((4, 4, 4, 8, 128), jnp.int32),
@@ -405,16 +428,22 @@
             pltpu.SemaphoreType.DMA((120,)),
             pltpu.SemaphoreType.DMA((8,)),
             pltpu.SemaphoreType.DMA((8,)),
-            pltpu.SemaphoreType.DMA((3,)),
+            pltpu.SemaphoreType.DMA((5,)),
         ],
         compiler_params=pltpu.CompilerParams(
-            collective_id=0, has_side_effects=True, vmem_limit_bytes=32 << 20
+            collective_id=0, has_side_effects=True, vmem_limit_bytes=55 << 20
         ),
         name="front",
-    )(hidden, gain, w_query, w_key, w_value, doc_ids, positions, inverse)
-
-
-def attend_kernel(bounds, q_ref, k_ref, v_ref, first_ref, out_ref, even, odd, summed):
+    )(
+        *(
+            pltpu.with_memory_space_constraint(a, pltpu.HBM)
+            for a in (hidden, gain, w_query, w_key, w_value, doc_ids, positions, inverse)
+        )
+    )
+
+
+def attend_kernel(bounds, q_ref, both_in, first_ref, out_ref, even, odd, summed):
+    both_ref = both_in.reshape(2, SEQUENCE, HEAD_SIZE)
     block = pl.program_id(0)
     t_low, t_clear, t_edge, t_high, row0 = (bounds[block, i] for i in range(5))
     scale = HEAD_SIZE ** (-0.5) * math.log2(math.e)
@@ -428,7 +457,7 @@
         peak = None
         for u in range(half // KEY_PIECE):
             first_key = begin + u * KEY_PIECE
-            keys = k_ref[pl.ds(pl.multiple_of(first_key, KEY_PIECE), KEY_PIECE), :]
+            keys = both_ref[0, pl.ds(pl.multiple_of(first_key, KEY_PIECE), KEY_PIECE), :]
             piece = lax.dot_general(
                 keys, queries, (((1,), (1,)), ((), ())), preferred_element_type=jnp.float32
             )
@@ -452,7 +481,7 @@
         for u in range(half // KEY_PIECE):
             weights = jnp.exp2(store[u * KEY_PIECE : (u + 1) * KEY_PIECE, :] * scale - offset)
             total = total + jnp.sum(weights.reshape(KEY_PIECE // 8, 8, width), axis=0)
-            values = v_ref[pl.ds(pl.multiple_of(begin + u * KEY_PIECE, KEY_PIECE), KEY_PIECE), :]
+            values = both_ref[1, pl.ds(pl.multiple_of(begin + u * KEY_PIECE, KEY_PIECE), KEY_PIECE), :]
             term = lax.dot_general(
                 values, weights.astype(jnp.bfloat16), (((0,), (0,)), ((), ())),
                 preferred_element_type=jnp.float32,
@@ -496,8 +525,7 @@
             grid=(4,),
             in_specs=[
                 pl.BlockSpec((1, BLOCK, 2 * HEAD_SIZE), lambda i, b: (i, 0, 0)),
-                pl.BlockSpec((None, SEQUENCE, HEAD_SIZE), lambda i, b: (0, 0, 0)),
-                pl.BlockSpec((None, SEQUENCE, HEAD_SIZE), lambda i, b: (1, 0, 0)),
+                pl.BlockSpec(memory_space=pltpu.VMEM),
                 pl.BlockSpec((1, 1, 2 * BLOCK), lambda i, b: (i, 0, 0)),
             ],
             out_specs=pl.BlockSpec((1, BLOCK, 2 * HEAD_SIZE), lambda i, b: (i, 0, 0)),
@@ -507,14 +535,14 @@
                 pltpu.VMEM((HEAD_SIZE, 2 * BLOCK), jnp.float32),
             ],
         ),
-        compiler_params=pltpu.CompilerParams(vmem_limit_bytes=48 << 20),
+        compiler_params=pltpu.CompilerParams(vmem_limit_bytes=16 << 20),
         name="attend",
-    )(bounds, queries, both, both, first)
+    )(bounds, queries, both, first)
 
 
 def back_kernel(
     own, w_out, hidden, out,
-    attended, weights, mine, given, landed, joined, arrived,
+    attended, mine, given, landed, joined, arrived,
     send_sems, recv_sems, local_sems, step_send, step_recv,
 ):
     x, y, zh, zl, c = place()
@@ -525,12 +553,6 @@
     pieces = 4
     width = 4096 // pieces
     cut = lambda i: pl.ds(i * width, width)
-    fetch = [
-        pltpu.make_async_copy(w_out.at[:, cut(i)], weights.at[:, cut(i)], local_sems.at[1 + i])
-        for i in range(pieces)
-    ]
-    for copy in fetch:
-        copy.start()
     greet(partners)
     spot = lambda j, cc: attended.at[:, pl.ds(pl.multiple_of((2 * j + cc) * 256, 256), 256)]
     copies = []
@@ -575,8 +597,7 @@
         to_across.append(cp.send(joined.at[i], arrived.at[i], across))
 
     for i in range(pieces):
-        fetch[i].wait()
-        term = jnp.dot(attended[...], weights[:, cut(i)], preferred_element_type=jnp.float32)
+        term = jnp.dot(attended[...], w_out[:, cut(i)], preferred_element_type=jnp.float32)
         term = term.reshape(2, 2, 48, width)
         mine[i] = jnp.where(c == 0, term[:, 0], term[:, 1])
         given[i] = jnp.where(c == 0, term[:, 1], term[:, 0]).astype(jnp.bfloat16)
@@ -601,11 +622,10 @@
     return pl.pallas_call(
         back_kernel,
         out_shape=jax.ShapeDtypeStruct((48, 4096), jnp.bfloat16),
-        in_specs=[anywhere, anywhere, inside],
+        in_specs=[anywhere, inside, inside],
         out_specs=inside,
         scratch_shapes=[
             pltpu.VMEM((BLOCK, 1024), jnp.bfloat16),
-            pltpu.VMEM((1024, 4096), jnp.bfloat16),
             pltpu.VMEM((4, 2, 48, 1024), jnp.float32),
             pltpu.VMEM((4, 2, 48, 1024), jnp.bfloat16),
             pltpu.VMEM((4, 2, 48, 1024), jnp.bfloat16),
@@ -613,7 +633,7 @@
             pltpu.VMEM((4, 48, 1024), jnp.bfloat16),
             pltpu.SemaphoreType.DMA((4,)),
             pltpu.SemaphoreType.DMA((4,)),
-            pltpu.SemaphoreType.DMA((5,)),
+            pltpu.SemaphoreType.DMA((1,)),
             pltpu.SemaphoreType.DMA((8,)),
             pltpu.SemaphoreType.DMA((8,)),
         ],
@@ -645,7 +665,8 @@
     t_high = (row0 + BLOCK - 1) // KEY_TILE + 1
     bounds = jnp.stack([t_low, t_clear, t_edge, t_high, row0], axis=1)
     lanes = jnp.concatenate([first, first], axis=1).reshape(4, 1, 2 * BLOCK)
-    attended = attend(bounds, queries, both.reshape(2, SEQUENCE, HEAD_SIZE), lanes)
+    both = pltpu.with_memory_space_constraint(both, pltpu.HBM)
+    attended = attend(bounds, queries, both, lanes)
     return back(attended, w_out, hidden_in)
 
 

time: 145 us -> 140 us (0.966); the launches traced: 143 us -> 140 us
  local copies, waits for them, and re-layouts: 10.1 us -> 5.91 us
  Pallas kernels: 132 us -> 134 us
    unnamed x23 -> x7, local copies, waits for them, and re-layouts: 9.97 us -> 5.12 us
    pallas_call x1, Pallas kernels: 79.6 us -> 82 us  [front(): pl.pallas_call(front_kernel, out_shape=(jax.ShapeDtypeStruct((4, BLOCK, 2...]
where the time goes in v3:
time: 140 us
  Pallas kernels  134 us (96%)
  local copies, waits for them, and re-layouts  5.91 us (4%)
    pallas_call x1, Pallas kernels, front(): pl.pallas_call(front_kernel, out_shape=(jax.ShapeDtypeStruct((4, BLOCK, 2...  82 us
    pallas_call x1, Pallas kernels, back(): pl.pallas_call(back_kernel, out_shape=jax.ShapeDtypeStruct((48, 4096), jn...  28.2 us
    pallas_call x1, Pallas kernels, attend(): pl.pallas_call(attend_kernel, out_shape=jax.ShapeDtypeStruct((4, BLOCK, 2...  23.5 us
    unnamed x7, local copies, waits for them, and re-layouts  5.12 us

profile of v3, /device:TPU:46, one launch (start us, length us, event | category | flops | bytes accessed | tf_op | source)
XLA Modules:
  0.0 139.8 jit_solution(17644441330880476841)
XLA Ops:
  0.0 0.0 copy-start.1
  0.0 82.0 %front.1 = (bf16[4,192,256]{2,1,0:T(8,128)(2,1)}, bf16[2,4,2,2,4,192,128]{6,5,4,3,2,1,0:T(8,128)(2,1)}, s32[8,128]{1,0:T(8,128)}) custom-call(bf16[48,4096]{1,0:T(8,128)(2,1)} %hidden.1, f32[1,4096]{1,0:T(1,128)} %bitcast.5, bf16[256,1024]{1,0:T(8,128)(2,1)} %w_query.1, bf16[256,256]{1,0:T(8,128)(2,1)} %w_key.1, bf16[256,256]{1,0:T(8,128)(2,1)} %w_value.1, ...), custom_call_target="tpu_custom_call" | custom-call | tf_op jit(solution)/shard_map/front/pallas_call | solution.py:404
  82.0 0.7 reshape.136
  82.7 0.1 pad_add_fusion
  82.8 0.1 fusion.5
  82.9 0.1 stack.2.bounds
  83.0 0.0 copy-start.2
  83.0 1.0 copy-done.2
  84.0 23.5 %attend.1.own = bf16[4,192,256]{2,1,0:T(8,128)(2,1)S(1)} custom-call(s32[4,5]{1,0:T(4,128)S(1)} %stack.2.bounds, bf16[4,192,256]{2,1,0:T(8,128)(2,1)S(1)} %copy-done.2, bf16[2,4,2,2,4,192,128]{6,5,4,3,2,1,0:T(8,128)(2,1)} %get-tuple-element.10.both_in, s32[4,1,384]{2,1,0:T(1,128)S(1)} %reshape.137.first_ref), custom_call_target="tpu_custom_call" | custom-call | tf_op jit(solution)/shard_map/attend/pallas_call | solution.py:520
  107.4 0.0 copy-done.1
  107.5 0.0 copy-start
  107.5 3.4 %copy-done = bf16[1024,4096]{1,0:T(8,128)(2,1)S(1)} copy-done((bf16[1024,4096]{1,0:T(8,128)(2,1)S(1)}, bf16[1024,4096]{1,0:T(8,128)(2,1)}, u32[]{:S(2)}) %copy-start) | copy-done | bytes 8388632
  110.8 28.2 %back.1 = bf16[48,4096]{1,0:T(8,128)(2,1)S(1)} custom-call(bf16[4,192,256]{2,1,0:T(8,128)(2,1)S(1)} %attend.1.own, bf16[1024,4096]{1,0:T(8,128)(2,1)S(1)} %copy-done, bf16[48,4096]{1,0:T(8,128)(2,1)S(1)} %copy-done.1), custom_call_target="tpu_custom_call" | custom-call | tf_op jit(solution)/shard_map/back/pallas_call | solution.py:622
  139.1 0.7 copy.11
  (3 shorter events, 0.0 us)
Async XLA Ops:
  0.0 107.4 %copy-start.1 = (bf16[48,4096]{1,0:T(8,128)(2,1)S(1)}, bf16[48,4096]{1,0:T(8,128)(2,1)}, u32[]{:S(2)}) copy-start(bf16[48,4096]{1,0:T(8,128)(2,1)} %hidden.1) | copy-start | bytes 1179652
  83.0 1.0 copy-start.2
  107.5 3.4 %copy-start = (bf16[1024,4096]{1,0:T(8,128)(2,1)S(1)}, bf16[1024,4096]{1,0:T(8,128)(2,1)}, u32[]{:S(2)}) copy-start(bf16[1024,4096]{1,0:T(8,128)(2,1)} %w_out.1) | copy-start | bytes 25165828

commit v4 on v3

--- a/solution.py
+++ b/solution.py
@@ -14,6 +14,7 @@
 KEY_TILE = 1024
 KEY_PIECE = 256
 MESH = pl.DeviceIdType.MESH
+FRONT_COPIES = 190
 
 
 rope_base = 500000.0
@@ -88,7 +89,8 @@
 def front_kernel(
     hidden_in, gain_in, w_query, w_key, w_value, doc_ids_in, positions_in, inverse_in,
     q_out, both, first_out,
-    hidden, gain, doc_ids, positions, inverse, rows, weights, meta, meta_own, tables, product, kv, q_sum,
+    hidden, gain, doc_ids, positions, inverse, rows, weights_q, weights_kv,
+    meta, meta_own, tables, product, kv, q_sum, q_own,
     send_sems, recv_sems, a2a_send, a2a_recv, local_sems,
 ):
     x, y, zh, zl, c = place()
@@ -106,6 +108,7 @@
     for partner in partners:
         pl.semaphore_signal(barrier, inc=1, device_id=partner, device_id_type=MESH)
     cp = Copies(send_sems, recv_sems)
+    same = lambda ref, target: cp.send(ref, ref, target)
     fetches = [
         pltpu.make_async_copy(source, target, local_sems.at[i])
         for i, (source, target) in enumerate(
@@ -136,73 +139,88 @@
     rows[p, c] = (widened * lax.rsqrt(power + norm_epsilon) * gain[...]).astype(jnp.bfloat16)
     pl.semaphore_wait(barrier, len(partners))
 
-    a2a = []
-    landing = (pl.ds(0, 256), pl.ds(256, 128))
-    for j in range(2):
-        for cc in range(2):
-            zt = 2 * c + j
-            own = (zt == zh) & (c == cc)
-            taken = pl.ds(pl.multiple_of(x * 64, 64), 64)
-            sources = (
-                w_query.at[taken, pl.ds(j * 512 + cc * 256, 256)],
-                (w_value if cc else w_key).at[taken, pl.ds(j * 128, 128)],
-            )
-            for i in range(2):
-                spot = weights.at[zh, y, x, :, landing[i]]
+    a2a = {0: [], 1: []}
+    stores = (weights_q, weights_kv)
+
+    def scatter_weights(i):
+        for j in range(2):
+            for cc in range(2):
+                zt = 2 * c + j
+                own = (zt == zh) & (c == cc)
+                taken = pl.ds(pl.multiple_of(x * 64, 64), 64)
+                if i == 0:
+                    source = w_query.at[taken, pl.ds(j * 512 + cc * 256, 256)]
+                else:
+                    source = (w_value if cc else w_key).at[taken, pl.ds(j * 128, 128)]
+                spot = stores[i].at[zh, y, x]
                 copy = pltpu.make_async_remote_copy(
-                    src_ref=sources[i],
+                    src_ref=source,
                     dst_ref=spot,
-                    send_sem=a2a_send.at[4 * j + 2 * cc + i],
-                    recv_sem=a2a_recv.at[2 * zh + i],
+                    send_sem=a2a_send.at[4 * i + 2 * j + cc],
+                    recv_sem=a2a_recv.at[4 * i + zh],
                     device_id=device(x, y, zt, zl, cc),
                     device_id_type=MESH,
                 )
-                stay = pltpu.make_async_copy(sources[i], spot, local_sems.at[i])
+                stay = pltpu.make_async_copy(source, spot, local_sems.at[i])
                 pl.when(own)(stay.start)
                 pl.when(jnp.logical_not(own))(copy.start)
-                a2a.append((own, copy, stay))
-    chunks_right = (pl.ds(0, 16), pl.ds(16, 32))
-    chunks_left = (pl.ds(32, 16), pl.ds(0, 32))
-    to_right, to_left, to_sibling = {}, {}, []
-    same = lambda ref, target: cp.send(ref, ref, target)
-    meta_z = [
-        cp.send(meta_own, meta.at[x, y, zh], device(x, y, (zh + k) % 4, zl, c)) for k in (1, 2, 3)
-    ]
-    for h in range(2):
-        to_right[0, h] = same(rows.at[p, c, chunks_right[h]], right)
-        to_left[0, h] = same(rows.at[p, c, chunks_left[h]], left)
-    to_sibling.append(same(rows.at[p, c], sibling))
-
-    for source in range(4):
-        for i in range(2):
+                a2a[i].append((own, copy, stay))
+
+    def collect_weights(i):
+        for source in range(4):
+            spot = stores[i].at[source, y, x]
             arrives = pltpu.make_async_remote_copy(
-                src_ref=weights.at[source, y, x, :, landing[i]],
-                dst_ref=weights.at[source, y, x, :, landing[i]],
+                src_ref=spot,
+                dst_ref=spot,
                 send_sem=a2a_send.at[0],
-                recv_sem=a2a_recv.at[2 * source + i],
+                recv_sem=a2a_recv.at[4 * i + source],
                 device_id=sibling,
                 device_id_type=MESH,
             )
             own = (zh == source) & (c == zh // 2)
             pl.when(jnp.logical_not(own))(arrives.wait_recv)
-    for own, copy, stay in a2a:
-        pl.when(own)(stay.wait)
-    mine = weights.at[:, y, x]
-    wy_next, wy_prev = same(mine, y_next), same(mine, y_prev)
-    wx, forwards = {}, []
-
-    def along_x(k):
-        piece = weights.at[:, ys[k], x]
-        wx[len(wx)] = (ys[k], same(piece, x_next), same(piece, x_prev))
-
-    def forward_x(k):
-        yy, a, b = wx[k]
+        for own, copy, stay in a2a[i]:
+            pl.when(own)(stay.wait)
+
+    wy, wy_far, wx, forwards = {}, {}, {0: {}, 1: {}}, {0: [], 1: []}
+
+    def along_y(i):
+        mine = stores[i].at[:, y, x]
+        wy[i] = same(mine, y_next), same(mine, y_prev)
+
+    def forward_y(i):
+        wy[i][0].wait_recv()
+        a = same(stores[i].at[pl.ds(0, 2), ys[3], x], y_next)
+        wy[i][1].wait_recv()
+        wy_far[i] = a, same(stores[i].at[pl.ds(2, 2), ys[1], x], y_prev)
+
+    def along_x(i, k):
+        piece = stores[i].at[:, ys[k], x]
+        wx[i][k] = same(piece, x_next), same(piece, x_prev)
+
+    def far_y(i):
+        for copy in wy_far[i]:
+            copy.wait_recv()
+        along_x(i, 2)
+
+    def forward_x(i, k):
+        a, b = wx[i][k]
         a.wait_recv()
-        forwards.append(same(weights.at[pl.ds(0, 2), yy, xs[3]], x_next))
+        forwards[i].append(same(stores[i].at[pl.ds(0, 2), ys[k], xs[3]], x_next))
         b.wait_recv()
-        forwards.append(same(weights.at[pl.ds(2, 2), yy, xs[1]], x_prev))
+        forwards[i].append(same(stores[i].at[pl.ds(2, 2), ys[k], xs[1]], x_prev))
+
+    chunks_right = (pl.ds(0, 16), pl.ds(16, 32))
+    chunks_left = (pl.ds(32, 16), pl.ds(0, 32))
+    to_right, to_left, to_sibling = {}, {}, {}
+
+    def far_spot(q, h, hop):
+        if h == 0:
+            return rows.at[q, c, pl.ds(0, 16) if hop == 7 else pl.ds(32, 16)]
+        return rows.at[q, c, pl.ds(16, 16), pl.ds(0 if hop == 7 else 2048, 2048)]
 
     def ring(step):
+        to_sibling[step] = []
         for h in range(2):
             for to, chunks, target, hop in (
                 (to_right, chunks_right, right, 7),
@@ -210,41 +228,14 @@
             ):
                 to[step, h].wait_recv()
                 q = (p + hop * (step + 1)) % 8
-                if step < 3:
-                    spot = rows.at[q, c, chunks[h]]
-                    to_sibling.append(same(spot, sibling))
-                    if step < 2:
-                        to[step + 1, h] = same(spot, target)
-                    else:
-                        to[3, h] = same(far_spot(q, h, hop), target)
-                else:
-                    to_sibling.append(same(far_spot(q, h, hop), sibling))
-
-    def far_spot(q, h, hop):
-        if h == 0:
-            return rows.at[q, c, pl.ds(0, 16) if hop == 7 else pl.ds(32, 16)]
-        return rows.at[q, c, pl.ds(16, 16), pl.ds(0 if hop == 7 else 2048, 2048)]
-
-    along_x(0)
-    for copy in meta_z:
-        copy.wait_recv()
-    mine = meta.at[x, y]
-    meta_y = [same(mine, target) for target in (y_next, y_far, y_prev)]
-    ring(0)
-    wy_next.wait_recv()
-    wy_far_next = same(weights.at[pl.ds(0, 2), ys[3], x], y_next)
-    along_x(3)
-    wy_prev.wait_recv()
-    wy_far_prev = same(weights.at[pl.ds(2, 2), ys[1], x], y_prev)
-    along_x(1)
-    for copy in meta_y:
-        copy.wait_recv()
-    mine = meta.at[x]
-    meta_x = [same(mine, target) for target in (x_next, x_far, x_prev)]
-    forward_x(0)
-    wy_far_next.wait_recv()
-    wy_far_prev.wait_recv()
-    along_x(2)
+                spot = rows.at[q, c, chunks[h]] if step < 3 else far_spot(q, h, hop)
+                if step < 2:
+                    to[step + 1, h] = same(spot, target)
+                elif step == 2:
+                    to[3, h] = same(far_spot(q, h, hop), target)
+                to_sibling[step].append(same(spot, sibling))
+
+    order = [zh, (zh + 3 + 2 * zl) % 4, (zh + 1 + 2 * zl) % 4, (zh + 2) % 4]
 
     def tables_of(zb):
         tile = meta[x, y, zb].astype(jnp.float32)
@@ -257,15 +248,175 @@
         tables[0, zb] = jnp.cos(angles) * attention_gain
         tables[1, zb] = jnp.where(lane < HEAD_SIZE // 2, -sine, sine)
 
-    tables_of(0)
-    tables_of(1)
+    def turn(head, cosine, sine):
+        return head * cosine + pltpu.roll(head, HEAD_SIZE // 2, 1) * sine
+
+    def multiply(zb, store, total):
+        total[...] = jnp.zeros_like(total)
+
+        @pl.loop(0, 4)
+        def _(k):
+            piece = store[k].reshape(1024, store.shape[-1])
+            depth = pl.ds(pl.multiple_of(k * 1024, 1024), 1024)
+            left_side = rows[pl.ds(2 * zb, 2), :, :, depth].reshape(BLOCK, 1024)
+            total[...] += jnp.dot(left_side, piece, preferred_element_type=jnp.float32)
+
+    q_stay = []
+
+    def queries_of(s):
+        zb = order[s]
+        multiply(zb, weights_q, q_sum)
+        for h in range(2):
+            at = pl.ds(h * HEAD_SIZE, HEAD_SIZE)
+            q_own[s, :, at] = turn(q_sum[:, at], tables[0, zb], tables[1, zb]).astype(jnp.bfloat16)
+        q_stay.append(pltpu.make_async_copy(q_own.at[s], q_out.at[zb], local_sems.at[5 + s]))
+        q_stay[-1].start()
+
+    halves = (pl.ds(0, 96), pl.ds(96, 96))
+    cell = lambda s, i, k: both.at[c, xs[i], order[s], ys[k]]
+    side = lambda s, i, k, f: both.at[c, xs[i], order[s], ys[k], halves[f]]
+    kx, kx_far, ky, ky_far, kv_stay, siblings = {}, {}, {}, {}, [], []
+    is_key = c == 0
+
+    def key_start(s):
+        zb = order[s]
+        for copy in to_sibling[s]:
+            copy.wait_recv()
+        multiply(zb, weights_kv, product)
+        cosine = jnp.where(is_key, tables[0, zb], 1.0)
+        sine = jnp.where(is_key, tables[1, zb], 0.0)
+        kv[s] = turn(product[...], cosine, sine).astype(jnp.bfloat16)
+        own, spot = kv.at[s], cell(s, 0, 0)
+        kx[s] = cp.send(own, spot, x_next), cp.send(own, spot, x_prev)
+        ky[s, 0] = cp.send(own, spot, y_next), cp.send(own, spot, y_prev)
+        siblings.append(cp.send(own, spot, sibling))
+        kv_stay.append(pltpu.make_async_copy(own, spot, local_sems.at[9 + s]))
+        kv_stay[-1].start()
+
+    def key_along_y(s, i):
+        ky[s, i] = same(cell(s, i, 0), y_next), same(cell(s, i, 0), y_prev)
+        siblings.append(same(cell(s, i, 0), sibling))
+
+    def key_x(s):
+        kx[s][0].wait_recv()
+        a = same(side(s, 3, 0, 0), x_next)
+        kx[s][1].wait_recv()
+        kx_far[s] = a, same(side(s, 1, 0, 1), x_prev)
+        key_along_y(s, 3)
+        key_along_y(s, 1)
+
+    def key_x_far(s):
+        for copy in kx_far[s]:
+            copy.wait_recv()
+        key_along_y(s, 2)
+
+    def key_y(s, i):
+        ky[s, i][0].wait_recv()
+        a = same(side(s, i, 3, 0), y_next)
+        ky[s, i][1].wait_recv()
+        ky_far[s, i] = a, same(side(s, i, 1, 1), y_prev)
+
+    def share(s, k):
+        siblings.append(same(both.at[c, :, order[s], ys[k]], sibling))
+
+    def key_y_rest(s):
+        key_y(s, 2)
+        share(s, 3)
+        share(s, 1)
+
+    def key_end(s):
+        for i in range(4):
+            for copy in ky_far[s, i]:
+                copy.wait_recv()
+        share(s, 2)
+
+    scatter_weights(1)
+    meta_z = [
+        cp.send(meta_own, meta.at[x, y, zh], device(x, y, (zh + k) % 4, zl, c)) for k in (1, 2, 3)
+    ]
+    for h in range(2):
+        to_right[0, h] = same(rows.at[p, c, chunks_right[h]], right)
+        to_left[0, h] = same(rows.at[p, c, chunks_left[h]], left)
+    scatter_weights(0)
+    own_to_sibling = same(rows.at[p, c], sibling)
+    collect_weights(1)
+    along_y(1)
+    along_x(1, 0)
+    forward_y(1)
+    along_x(1, 3)
+    along_x(1, 1)
+    collect_weights(0)
+    along_y(0)
+    for copy in meta_z:
+        copy.wait_recv()
+    mine = meta.at[x, y]
+    meta_y = [same(mine, target) for target in (y_next, y_far, y_prev)]
+    forward_x(1, 0)
+    far_y(1)
+    tables_of(order[0])
+    ring(0)
+    forward_x(1, 3)
+    forward_x(1, 1)
+    along_x(0, 0)
+    forward_y(0)
+    along_x(0, 3)
+    along_x(0, 1)
+    forward_x(1, 2)
+    far_y(0)
+    tables_of(order[1])
+    for copy in forwards[1]:
+        copy.wait_recv()
+    own_to_sibling.wait_recv()
+    key_start(0)
+    for copy in meta_y:
+        copy.wait_recv()
+    mine = meta.at[x]
+    meta_x = [same(mine, target) for target in (x_next, x_far, x_prev)]
+    tables_of(order[2])
     ring(1)
-    tables_of(2)
-    forward_x(1)
-    forward_x(2)
-    tables_of(3)
+    key_x(0)
+    forward_x(0, 0)
+    key_start(1)
+    key_y(0, 0)
+    key_x_far(0)
+    forward_x(0, 3)
+    tables_of(order[3])
+    key_x(1)
+    key_y(0, 3)
+    key_y(0, 1)
+    forward_x(0, 1)
     ring(2)
-    forward_x(3)
+    key_y(1, 0)
+    key_x_far(1)
+    key_y_rest(0)
+    key_start(2)
+    forward_x(0, 2)
+    key_y(1, 3)
+    key_y(1, 1)
+    key_end(0)
+    key_x(2)
+    key_y_rest(1)
+    key_y(2, 0)
+    key_x_far(2)
+    for copy in forwards[0]:
+        copy.wait_recv()
+    queries_of(0)
+    ring(3)
+    key_y(2, 3)
+    key_y(2, 1)
+    key_start(3)
+    key_end(1)
+    key_y_rest(2)
+    queries_of(1)
+    key_x(3)
+    key_y(3, 0)
+    key_end(2)
+    queries_of(2)
+    key_x_far(3)
+    key_y(3, 3)
+    key_y(3, 1)
+    queries_of(3)
+    key_y_rest(3)
     for copy in meta_x:
         copy.wait_recv()
     everything = meta[...].reshape(64, 8, 128)
@@ -281,121 +432,16 @@
         for d in range(1, 6):
             first = jnp.where(documents == d, firsts[d - 1], first)
         first_out[2 * zb : 2 * zb + 2, :] = first.astype(jnp.int32)
-    ring(3)
-    for copy in forwards + to_sibling:
-        copy.wait_recv()
-
-    def depth(k):
-        return pl.ds(pl.multiple_of(k * 256, 256), 256)
-
-    product[...] = jnp.zeros_like(product)
-
-    @pl.loop(0, 16)
-    def _(k):
-        piece = weights[k // 4, k % 4, :, :, 256:384].reshape(256, HEAD_SIZE)
-        left_side = rows[:, :, :, depth(k)].reshape(768, 256)
-        product[...] += jnp.dot(left_side, piece, preferred_element_type=jnp.float32)
-
-    def turn(head, cosine, sine):
-        return head * cosine + pltpu.roll(head, HEAD_SIZE // 2, 1) * sine
-
-    is_key = c == 0
-    for zb in range(4):
-        head = product[zb * BLOCK : (zb + 1) * BLOCK, :]
-        cosine = jnp.where(is_key, tables[0, zb], 1.0)
-        sine = jnp.where(is_key, tables[1, zb], 0.0)
-        kv[zb // 2, zb % 2] = turn(head, cosine, sine).astype(jnp.bfloat16)
-
-    whole = lambda xx, yy: both.at[c, xx, :, :, yy]
-    half = lambda f, xx, yy: both.at[c, xx, f, :, yy]
-    part = lambda a, xx, yy: both.at[c, xx, :, a, yy]
-    cell = lambda f, a, xx, yy: both.at[c, xx, f, a, yy]
-    from_y_prev = cp.send(kv, whole(x, y), y_next)
-    from_x_prev = cp.send(kv, whole(x, y), x_next)
-    from_y_next = cp.send(kv, whole(x, y), y_prev)
-    from_x_next = cp.send(kv, whole(x, y), x_prev)
-    siblings = [cp.send(kv, whole(x, y), sibling)]
-    stay = pltpu.make_async_copy(kv, whole(x, y), local_sems.at[2])
-    stay.start()
-
-    def queries_of(zb):
-        q_sum[...] = jnp.zeros_like(q_sum)
-
-        @pl.loop(0, 16)
-        def _(k):
-            piece = weights[k // 4, k % 4, :, :, 0:256].reshape(256, 256)
-            left_side = rows[2 * zb : 2 * zb + 2, :, :, depth(k)].reshape(BLOCK, 256)
-            q_sum[...] += jnp.dot(left_side, piece, preferred_element_type=jnp.float32)
-
-        for h in range(2):
-            at = pl.ds(h * HEAD_SIZE, HEAD_SIZE)
-            q_out[zb, :, at] = turn(q_sum[:, at], tables[0, zb], tables[1, zb]).astype(jnp.bfloat16)
-
-    def share(xx, yy):
-        siblings.append(same(whole(xx, yy), sibling))
-
-    a_prev, a_next, b_prev, b_next = {}, {}, {}, {}
-
-    def a_send(k):
-        a_prev[k] = same(part(0, x, ys[k]), x_next)
-        a_next[k] = same(part(0, x, ys[k]), x_prev)
-
-    def b_send(k):
-        b_prev[k] = same(part(1, xs[k], y), y_next)
-        b_next[k] = same(part(1, xs[k], y), y_prev)
-
-    queries_of(0)
-    queries_of(1)
-    from_y_prev.wait_recv()
-    y_far_prev = same(half(0, x, ys[3]), y_next)
-    a_send(3)
-    from_x_prev.wait_recv()
-    x_far_prev = same(half(0, xs[3], y), x_next)
-    b_send(3)
-    from_y_next.wait_recv()
-    y_far_next = same(half(1, x, ys[1]), y_prev)
-    a_send(1)
-    from_x_next.wait_recv()
-    x_far_next = same(half(1, xs[1], y), x_prev)
-    b_send(1)
-    for xx, yy in ((0, 3), (0, 1), (3, 0), (1, 0)):
-        share(xs[xx], ys[yy])
-    queries_of(2)
-    y_far_prev.wait_recv()
-    y_far_next.wait_recv()
-    a_send(2)
-    x_far_prev.wait_recv()
-    x_far_next.wait_recv()
-    b_send(2)
-    share(x, ys[2])
-    share(xs[2], y)
-    fa, fb = {}, {}
-    for k in (3, 1, 2):
-        a_prev[k].wait_recv()
-        fa[k, 0] = same(cell(0, 0, xs[3], ys[k]), x_next)
-        b_prev[k].wait_recv()
-        fb[k, 0] = same(cell(0, 1, xs[k], ys[3]), y_next)
-        a_next[k].wait_recv()
-        fa[k, 1] = same(cell(1, 0, xs[1], ys[k]), x_prev)
-        b_next[k].wait_recv()
-        fb[k, 1] = same(cell(1, 1, xs[k], ys[1]), y_prev)
-        if k == 1:
-            for xx in (1, 3):
-                for yy in (1, 3):
-                    share(xs[xx], ys[yy])
-            queries_of(3)
-    for k in (3, 1, 2):
-        for f in range(2):
-            fa[k, f].wait_recv()
-            fb[k, f].wait_recv()
-    for xx, yy in ((1, 2), (3, 2), (2, 1), (2, 3), (2, 2)):
-        share(xs[xx], ys[yy])
+    key_end(3)
     for copy in siblings:
         copy.wait_recv()
-    stay.wait()
-    for own, copy, _ in a2a:
-        pl.when(jnp.logical_not(own))(copy.wait_send)
+    for copy in q_stay + kv_stay:
+        copy.wait()
+    for i in range(2):
+        for own, copy, _ in a2a[i]:
+            pl.when(jnp.logical_not(own))(copy.wait_send)
     cp.finish()
+    assert cp.count == FRONT_COPIES, cp.count
 
 
 def front(hidden, gain, w_query, w_key, w_value, doc_ids, positions, inverse):
@@ -405,11 +451,11 @@
         front_kernel,
         out_shape=(
             jax.ShapeDtypeStruct((4, BLOCK, 2 * HEAD_SIZE), jnp.bfloat16),
-            jax.ShapeDtypeStruct((2, 4, 2, 2, 4, BLOCK, HEAD_SIZE), jnp.bfloat16),
+            jax.ShapeDtypeStruct((2, 4, 4, 4, BLOCK, HEAD_SIZE), jnp.bfloat16),
             jax.ShapeDtypeStruct((8, 128), jnp.int32),
         ),
         in_specs=[outside] * 8,
-        out_specs=(inside, outside, inside),
+        out_specs=(outside, outside, inside),
         scratch_shapes=[
             pltpu.VMEM((48, 4096), jnp.bfloat16),
             pltpu.VMEM((1, 4096), jnp.float32),
@@ -417,18 +463,20 @@
             pltpu.VMEM((1, BLOCK), jnp.int32),
             pltpu.VMEM((1, HEAD_SIZE), jnp.float32),
             pltpu.VMEM((8, 2, 48, 4096), jnp.bfloat16),
-            pltpu.VMEM((4, 4, 4, 64, 384), jnp.bfloat16),
+            pltpu.VMEM((4, 4, 4, 64, 256), jnp.bfloat16),
+            pltpu.VMEM((4, 4, 4, 64, 128), jnp.bfloat16),
             pltpu.VMEM((4, 4, 4, 8, 128), jnp.int32),
             pltpu.VMEM((8, 128), jnp.int32),
             pltpu.VMEM((2, 4, BLOCK, HEAD_SIZE), jnp.float32),
-            pltpu.VMEM((768, HEAD_SIZE), jnp.float32),
-            pltpu.VMEM((2, 2, BLOCK, HEAD_SIZE), jnp.bfloat16),
+            pltpu.VMEM((BLOCK, HEAD_SIZE), jnp.float32),
+            pltpu.VMEM((4, BLOCK, HEAD_SIZE), jnp.bfloat16),
             pltpu.VMEM((BLOCK, 2 * HEAD_SIZE), jnp.float32),
-            pltpu.SemaphoreType.DMA((120,)),
-            pltpu.SemaphoreType.DMA((120,)),
+            pltpu.VMEM((4, BLOCK, 2 * HEAD_SIZE), jnp.bfloat16),
+            pltpu.SemaphoreType.DMA((FRONT_COPIES,)),
+            pltpu.SemaphoreType.DMA((FRONT_COPIES,)),
             pltpu.SemaphoreType.DMA((8,)),
             pltpu.SemaphoreType.DMA((8,)),
-            pltpu.SemaphoreType.DMA((5,)),
+            pltpu.SemaphoreType.DMA((13,)),
         ],
         compiler_params=pltpu.CompilerParams(
             collective_id=0, has_side_effects=True, vmem_limit_bytes=55 << 20
@@ -542,7 +590,7 @@
 
 def back_kernel(
     own, w_out, hidden, out,
-    attended, mine, given, landed, joined, arrived,
+    attended, weights, mine, given, landed, joined, arrived,
     send_sems, recv_sems, local_sems, step_send, step_recv,
 ):
     x, y, zh, zl, c = place()
@@ -553,6 +601,12 @@
     pieces = 4
     width = 4096 // pieces
     cut = lambda i: pl.ds(i * width, width)
+    fetch = [
+        pltpu.make_async_copy(w_out.at[:, cut(i)], weights.at[:, cut(i)], local_sems.at[1 + i])
+        for i in range(pieces)
+    ]
+    for copy in fetch:
+        copy.start()
     greet(partners)
     spot = lambda j, cc: attended.at[:, pl.ds(pl.multiple_of((2 * j + cc) * 256, 256), 256)]
     copies = []
@@ -597,7 +651,8 @@
         to_across.append(cp.send(joined.at[i], arrived.at[i], across))
 
     for i in range(pieces):
-        term = jnp.dot(attended[...], w_out[:, cut(i)], preferred_element_type=jnp.float32)
+        fetch[i].wait()
+        term = jnp.dot(attended[...], weights[:, cut(i)], preferred_element_type=jnp.float32)
         term = term.reshape(2, 2, 48, width)
         mine[i] = jnp.where(c == 0, term[:, 0], term[:, 1])
         given[i] = jnp.where(c == 0, term[:, 1], term[:, 0]).astype(jnp.bfloat16)
@@ -622,10 +677,11 @@
     return pl.pallas_call(
         back_kernel,
         out_shape=jax.ShapeDtypeStruct((48, 4096), jnp.bfloat16),
-        in_specs=[anywhere, inside, inside],
+        in_specs=[anywhere, anywhere, inside],
         out_specs=inside,
         scratch_shapes=[
             pltpu.VMEM((BLOCK, 1024), jnp.bfloat16),
+            pltpu.VMEM((1024, 4096), jnp.bfloat16),
             pltpu.VMEM((4, 2, 48, 1024), jnp.float32),
             pltpu.VMEM((4, 2, 48, 1024), jnp.bfloat16),
             pltpu.VMEM((4, 2, 48, 1024), jnp.bfloat16),
@@ -633,7 +689,7 @@
             pltpu.VMEM((4, 48, 1024), jnp.bfloat16),
             pltpu.SemaphoreType.DMA((4,)),
             pltpu.SemaphoreType.DMA((4,)),
-            pltpu.SemaphoreType.DMA((1,)),
+            pltpu.SemaphoreType.DMA((5,)),
             pltpu.SemaphoreType.DMA((8,)),
             pltpu.SemaphoreType.DMA((8,)),
         ],
@@ -665,7 +721,9 @@
     t_high = (row0 + BLOCK - 1) // KEY_TILE + 1
     bounds = jnp.stack([t_low, t_clear, t_edge, t_high, row0], axis=1)
     lanes = jnp.concatenate([first, first], axis=1).reshape(4, 1, 2 * BLOCK)
-    both = pltpu.with_memory_space_constraint(both, pltpu.HBM)
+    queries, both, w_out = (
+        pltpu.with_memory_space_constraint(a, pltpu.HBM) for a in (queries, both, w_out)
+    )
     attended = attend(bounds, queries, both, lanes)
     return back(attended, w_out, hidden_in)
 

time: 140 us -> 137 us (0.979)
  local copies, waits for them, and re-layouts: 5.91 us -> 1.55 us
    unnamed x7 -> x3, local copies, waits for them, and re-layouts: 5.12 us -> 0.75 us
    pallas_call x1, Pallas kernels: 82 us -> 85.9 us  [front(): pl.pallas_call(front_kernel, out_shape=(jax.ShapeDtypeStruct((4, BLOCK, 2...]
    pallas_call x1, Pallas kernels: 23.5 us -> 20.5 us  [attend(): pl.pallas_call(attend_kernel, out_shape=jax.ShapeDtypeStruct((4, BLOCK, 2...]
where the time goes in v4:
time: 137 us; the launch traced here: 136 us
  Pallas kernels  134 us (98%)
  local copies, waits for them, and re-layouts  1.55 us (1%)
    pallas_call x1, Pallas kernels, front(): pl.pallas_call(front_kernel, out_shape=(jax.ShapeDtypeStruct((4, BLOCK, 2...  85.9 us
    pallas_call x1, Pallas kernels, back(): pl.pallas_call(back_kernel, out_shape=jax.ShapeDtypeStruct((48, 4096), jn...  27.8 us
    pallas_call x1, Pallas kernels, attend(): pl.pallas_call(attend_kernel, out_shape=jax.ShapeDtypeStruct((4, BLOCK, 2...  20.5 us

profile of v4, /device:TPU:46, one launch (start us, length us, event | category | flops | bytes accessed | tf_op | source)
XLA Modules:
  0.0 136.0 jit_solution(483951877505580780)
XLA Ops:
  0.0 0.0 copy-start
  0.0 85.9 %front.1 = (bf16[4,192,256]{2,1,0:T(8,128)(2,1)}, bf16[2,4,4,4,192,128]{5,4,3,2,1,0:T(8,128)(2,1)}, s32[8,128]{1,0:T(8,128)}) custom-call(bf16[48,4096]{1,0:T(8,128)(2,1)} %hidden.1, f32[1,4096]{1,0:T(1,128)} %bitcast.5, bf16[256,1024]{1,0:T(8,128)(2,1)} %w_query.1, bf16[256,256]{1,0:T(8,128)(2,1)} %w_key.1, bf16[256,256]{1,0:T(8,128)(2,1)} %w_value.1, ...), custom_call_target="tpu_custom_call" | custom-call | tf_op jit(solution)/shard_map/front/pallas_call | solution.py:450
  85.9 0.7 reshape.136
  86.6 0.1 pad_add_fusion
  86.7 0.1 fusion.5
  86.8 0.1 stack.2.bounds
  86.9 20.5 %attend.1.own = bf16[4,192,256]{2,1,0:T(8,128)(2,1)S(1)} custom-call(s32[4,5]{1,0:T(4,128)S(1)} %stack.2.bounds, bf16[4,192,256]{2,1,0:T(8,128)(2,1)} %get-tuple-element.9.q_ref, bf16[2,4,4,4,192,128]{5,4,3,2,1,0:T(8,128)(2,1)} %get-tuple-element.10.both_in, s32[4,1,384]{2,1,0:T(1,128)S(1)} %reshape.137.first_ref), custom_call_target="tpu_custom_call" | custom-call | tf_op jit(solution)/shard_map/attend/pallas_call | solution.py:568
  107.4 0.0 copy-done
  107.4 27.8 %back.1 = bf16[48,4096]{1,0:T(8,128)(2,1)S(1)} custom-call(bf16[4,192,256]{2,1,0:T(8,128)(2,1)S(1)} %attend.1.own, bf16[1024,4096]{1,0:T(8,128)(2,1)} %w_out.1, bf16[48,4096]{1,0:T(8,128)(2,1)S(1)} %copy-done), custom_call_target="tpu_custom_call" | custom-call | tf_op jit(solution)/shard_map/back/pallas_call | solution.py:677
  135.2 0.7 copy.11
  (3 shorter events, 0.0 us)
Async XLA Ops:
  0.0 107.4 %copy-start = (bf16[48,4096]{1,0:T(8,128)(2,1)S(1)}, bf16[48,4096]{1,0:T(8,128)(2,1)}, u32[]{:S(2)}) copy-start(bf16[48,4096]{1,0:T(8,128)(2,1)} %hidden.1) | copy-start | bytes 1179652

commit v5 on v4

--- a/solution.py
+++ b/solution.py
@@ -182,58 +182,80 @@
         for own, copy, stay in a2a[i]:
             pl.when(own)(stay.wait)
 
-    wy, wy_far, wx, forwards = {}, {}, {0: {}, 1: {}}, {0: [], 1: []}
+    wy, wy_far, wx, forwards = {}, {}, {}, {0: [], 1: []}
 
     def along_y(i):
         mine = stores[i].at[:, y, x]
         wy[i] = same(mine, y_next), same(mine, y_prev)
 
-    def forward_y(i):
-        wy[i][0].wait_recv()
-        a = same(stores[i].at[pl.ds(0, 2), ys[3], x], y_next)
-        wy[i][1].wait_recv()
-        wy_far[i] = a, same(stores[i].at[pl.ds(2, 2), ys[1], x], y_prev)
+    def forward_y(i, side):
+        wy[i][side].wait_recv()
+        spot = stores[i].at[pl.ds(2 * side, 2), ys[3 - 2 * side], x]
+        wy_far[i, side] = same(spot, (y_next, y_prev)[side])
 
     def along_x(i, k):
         piece = stores[i].at[:, ys[k], x]
-        wx[i][k] = same(piece, x_next), same(piece, x_prev)
+        wx[i, k] = same(piece, x_next), same(piece, x_prev)
 
     def far_y(i):
-        for copy in wy_far[i]:
-            copy.wait_recv()
+        wy_far[i, 0].wait_recv()
+        wy_far[i, 1].wait_recv()
         along_x(i, 2)
 
-    def forward_x(i, k):
-        a, b = wx[i][k]
-        a.wait_recv()
-        forwards[i].append(same(stores[i].at[pl.ds(0, 2), ys[k], xs[3]], x_next))
-        b.wait_recv()
-        forwards[i].append(same(stores[i].at[pl.ds(2, 2), ys[k], xs[1]], x_prev))
+    def forward_x(i, k, side):
+        wx[i, k][side].wait_recv()
+        spot = stores[i].at[pl.ds(2 * side, 2), ys[k], xs[3 - 2 * side]]
+        forwards[i].append(same(spot, (x_next, x_prev)[side]))
 
     chunks_right = (pl.ds(0, 16), pl.ds(16, 32))
     chunks_left = (pl.ds(32, 16), pl.ds(0, 32))
-    to_right, to_left, to_sibling = {}, {}, {}
+    to_right, to_left, to_sibling, own_row = {}, {}, {k: [] for k in range(4)}, []
 
     def far_spot(q, h, hop):
         if h == 0:
             return rows.at[q, c, pl.ds(0, 16) if hop == 7 else pl.ds(32, 16)]
         return rows.at[q, c, pl.ds(16, 16), pl.ds(0 if hop == 7 else 2048, 2048)]
 
-    def ring(step):
-        to_sibling[step] = []
-        for h in range(2):
-            for to, chunks, target, hop in (
-                (to_right, chunks_right, right, 7),
-                (to_left, chunks_left, left, 1),
-            ):
-                to[step, h].wait_recv()
-                q = (p + hop * (step + 1)) % 8
-                spot = rows.at[q, c, chunks[h]] if step < 3 else far_spot(q, h, hop)
-                if step < 2:
-                    to[step + 1, h] = same(spot, target)
-                elif step == 2:
-                    to[3, h] = same(far_spot(q, h, hop), target)
-                to_sibling[step].append(same(spot, sibling))
+    def ring_start(h):
+        to_right[0, h] = same(rows.at[p, c, chunks_right[h]], right)
+        to_left[0, h] = same(rows.at[p, c, chunks_left[h]], left)
+
+    def own_start():
+        own_row.append(same(rows.at[p, c], sibling))
+
+    def ring(step, h, side):
+        to, chunks, target, hop = (
+            (to_right, chunks_right, right, 7),
+            (to_left, chunks_left, left, 1),
+        )[side]
+        to[step, h].wait_recv()
+        q = (p + hop * (step + 1)) % 8
+        spot = rows.at[q, c, chunks[h]] if step < 3 else far_spot(q, h, hop)
+        if step < 2:
+            to[step + 1, h] = same(spot, target)
+        elif step == 2:
+            to[3, h] = same(far_spot(q, h, hop), target)
+        to_sibling[step].append(same(spot, sibling))
+
+    metas = {}
+
+    def meta_start():
+        metas[0] = [
+            cp.send(meta_own, meta.at[x, y, zh], device(x, y, (zh + k) % 4, zl, c))
+            for k in (1, 2, 3)
+        ]
+
+    def meta_along_y():
+        for copy in metas[0]:
+            copy.wait_recv()
+        mine = meta.at[x, y]
+        metas[1] = [same(mine, target) for target in (y_next, y_far, y_prev)]
+
+    def meta_along_x():
+        for copy in metas[1]:
+            copy.wait_recv()
+        mine = meta.at[x]
+        metas[2] = [same(mine, target) for target in (x_next, x_far, x_prev)]
 
     order = [zh, (zh + 3 + 2 * zl) % 4, (zh + 1 + 2 * zl) % 4, (zh + 2) % 4]
 
@@ -265,6 +287,9 @@
 
     def queries_of(s):
         zb = order[s]
+        if not q_stay:
+            for copy in forwards[0]:
+                copy.wait_recv()
         multiply(zb, weights_q, q_sum)
         for h in range(2):
             at = pl.ds(h * HEAD_SIZE, HEAD_SIZE)
@@ -274,13 +299,13 @@
 
     halves = (pl.ds(0, 96), pl.ds(96, 96))
     cell = lambda s, i, k: both.at[c, xs[i], order[s], ys[k]]
-    side = lambda s, i, k, f: both.at[c, xs[i], order[s], ys[k], halves[f]]
+    side_of = lambda s, i, k, f: both.at[c, xs[i], order[s], ys[k], halves[f]]
     kx, kx_far, ky, ky_far, kv_stay, siblings = {}, {}, {}, {}, [], []
     is_key = c == 0
 
     def key_start(s):
         zb = order[s]
-        for copy in to_sibling[s]:
+        for copy in to_sibling[s] + (forwards[1] + own_row if s == 0 else []):
             copy.wait_recv()
         multiply(zb, weights_kv, product)
         cosine = jnp.where(is_key, tables[0, zb], 1.0)
@@ -297,127 +322,155 @@
         ky[s, i] = same(cell(s, i, 0), y_next), same(cell(s, i, 0), y_prev)
         siblings.append(same(cell(s, i, 0), sibling))
 
-    def key_x(s):
-        kx[s][0].wait_recv()
-        a = same(side(s, 3, 0, 0), x_next)
-        kx[s][1].wait_recv()
-        kx_far[s] = a, same(side(s, 1, 0, 1), x_prev)
-        key_along_y(s, 3)
-        key_along_y(s, 1)
+    def key_x(s, side):
+        kx[s][side].wait_recv()
+        spot = side_of(s, 3 - 2 * side, 0, side)
+        kx_far[s, side] = same(spot, (x_next, x_prev)[side])
+        key_along_y(s, 3 - 2 * side)
 
     def key_x_far(s):
-        for copy in kx_far[s]:
-            copy.wait_recv()
+        kx_far[s, 0].wait_recv()
+        kx_far[s, 1].wait_recv()
         key_along_y(s, 2)
 
-    def key_y(s, i):
-        ky[s, i][0].wait_recv()
-        a = same(side(s, i, 3, 0), y_next)
-        ky[s, i][1].wait_recv()
-        ky_far[s, i] = a, same(side(s, i, 1, 1), y_prev)
+    def key_y(s, i, side):
+        ky[s, i][side].wait_recv()
+        spot = side_of(s, i, 3 - 2 * side, side)
+        ky_far[s, i, side] = same(spot, (y_next, y_prev)[side])
 
     def share(s, k):
         siblings.append(same(both.at[c, :, order[s], ys[k]], sibling))
 
-    def key_y_rest(s):
-        key_y(s, 2)
-        share(s, 3)
-        share(s, 1)
-
     def key_end(s):
         for i in range(4):
-            for copy in ky_far[s, i]:
-                copy.wait_recv()
+            for side in range(2):
+                ky_far[s, i, side].wait_recv()
         share(s, 2)
 
     scatter_weights(1)
-    meta_z = [
-        cp.send(meta_own, meta.at[x, y, zh], device(x, y, (zh + k) % 4, zl, c)) for k in (1, 2, 3)
-    ]
-    for h in range(2):
-        to_right[0, h] = same(rows.at[p, c, chunks_right[h]], right)
-        to_left[0, h] = same(rows.at[p, c, chunks_left[h]], left)
+    meta_start()
     scatter_weights(0)
-    own_to_sibling = same(rows.at[p, c], sibling)
+    ring_start(0)
+    ring_start(1)
     collect_weights(1)
     along_y(1)
     along_x(1, 0)
-    forward_y(1)
+    forward_y(1, 0)
+    own_start()
     along_x(1, 3)
+    collect_weights(0)
+    ring(0, 0, 0)
+    forward_x(1, 0, 1)
+    forward_y(1, 1)
     along_x(1, 1)
-    collect_weights(0)
+    forward_x(1, 0, 0)
     along_y(0)
-    for copy in meta_z:
-        copy.wait_recv()
-    mine = meta.at[x, y]
-    meta_y = [same(mine, target) for target in (y_next, y_far, y_prev)]
-    forward_x(1, 0)
+    meta_along_y()
+    ring(0, 0, 1)
+    forward_x(1, 3, 1)
     far_y(1)
+    ring(0, 1, 0)
+    along_x(0, 0)
+    forward_x(1, 2, 0)
+    forward_x(1, 1, 0)
+    forward_y(0, 1)
+    forward_x(1, 3, 0)
+    ring(1, 0, 0)
+    ring(0, 1, 1)
+    forward_x(1, 1, 1)
+    forward_x(1, 2, 1)
+    along_x(0, 1)
     tables_of(order[0])
-    ring(0)
-    forward_x(1, 3)
-    forward_x(1, 1)
-    along_x(0, 0)
-    forward_y(0)
+    forward_y(0, 0)
+    ring(1, 0, 1)
+    tables_of(order[1])
+    key_start(0)
+    ring(1, 1, 0)
+    far_y(0)
     along_x(0, 3)
-    along_x(0, 1)
-    forward_x(1, 2)
-    far_y(0)
-    tables_of(order[1])
-    for copy in forwards[1]:
-        copy.wait_recv()
-    own_to_sibling.wait_recv()
-    key_start(0)
-    for copy in meta_y:
-        copy.wait_recv()
-    mine = meta.at[x]
-    meta_x = [same(mine, target) for target in (x_next, x_far, x_prev)]
+    key_y(0, 0, 0)
+    ring(2, 0, 0)
+    ring(1, 1, 1)
+    key_x(0, 0)
+    key_x(0, 1)
+    key_y(0, 0, 1)
+    key_start(1)
+    key_y(0, 3, 0)
+    ring(2, 1, 0)
+    forward_x(0, 3, 0)
+    forward_x(0, 1, 1)
+    ring(2, 0, 1)
+    key_y(0, 1, 1)
+    key_x_far(0)
+    key_x(1, 0)
+    key_x(1, 1)
+    ring(2, 1, 1)
+    key_y(0, 1, 0)
+    key_y(0, 3, 1)
+    key_y(1, 0, 1)
+    ring(3, 0, 0)
     tables_of(order[2])
-    ring(1)
-    key_x(0)
-    forward_x(0, 0)
-    key_start(1)
-    key_y(0, 0)
-    key_x_far(0)
-    forward_x(0, 3)
+    forward_x(0, 2, 1)
+    key_x_far(1)
+    key_y(0, 2, 0)
+    key_y(0, 2, 1)
+    forward_x(0, 1, 0)
+    key_y(1, 3, 0)
+    key_start(2)
+    forward_x(0, 0, 0)
+    key_y(1, 1, 0)
+    ring(3, 1, 0)
+    key_y(1, 3, 1)
+    ring(3, 1, 1)
+    key_y(1, 2, 0)
+    forward_x(0, 3, 1)
+    key_y(1, 1, 1)
+    ring(3, 0, 1)
+    key_y(1, 2, 1)
+    key_y(1, 0, 0)
     tables_of(order[3])
-    key_x(1)
-    key_y(0, 3)
-    key_y(0, 1)
-    forward_x(0, 1)
-    ring(2)
-    key_y(1, 0)
-    key_x_far(1)
-    key_y_rest(0)
-    key_start(2)
-    forward_x(0, 2)
-    key_y(1, 3)
-    key_y(1, 1)
+    share(0, 1)
+    key_x(2, 0)
+    key_x(2, 1)
+    key_start(3)
+    forward_x(0, 2, 0)
+    key_x_far(2)
+    key_y(2, 0, 1)
+    forward_x(0, 0, 1)
+    key_end(1)
+    share(1, 1)
+    key_x(3, 0)
+    key_y(2, 1, 0)
+    key_x(3, 1)
+    share(1, 3)
     key_end(0)
-    key_x(2)
-    key_y_rest(1)
-    key_y(2, 0)
-    key_x_far(2)
-    for copy in forwards[0]:
-        copy.wait_recv()
+    share(0, 3)
+    key_y(2, 2, 1)
+    key_x_far(3)
+    key_y(2, 3, 1)
+    key_y(2, 0, 0)
+    key_y(2, 2, 0)
+    key_y(2, 3, 0)
+    key_y(2, 1, 1)
+    share(2, 3)
+    queries_of(2)
+    key_y(3, 0, 0)
+    key_y(3, 3, 1)
+    queries_of(1)
+    share(2, 1)
+    key_y(3, 2, 0)
+    meta_along_x()
+    key_y(3, 1, 1)
+    key_y(3, 2, 1)
+    key_y(3, 0, 1)
+    key_y(3, 1, 0)
+    key_y(3, 3, 0)
+    share(3, 3)
+    share(3, 1)
     queries_of(0)
-    ring(3)
-    key_y(2, 3)
-    key_y(2, 1)
-    key_start(3)
-    key_end(1)
-    key_y_rest(2)
-    queries_of(1)
-    key_x(3)
-    key_y(3, 0)
     key_end(2)
-    queries_of(2)
-    key_x_far(3)
-    key_y(3, 3)
-    key_y(3, 1)
     queries_of(3)
-    key_y_rest(3)
-    for copy in meta_x:
+    for copy in metas[2]:
         copy.wait_recv()
     everything = meta[...].reshape(64, 8, 128)
     line = lax.broadcasted_iota(jnp.int32, (8, 128), 0)

time: 137 us -> 122 us (0.89)
  the two profiles are of different devices: /device:TPU:46 before, /device:TPU:10 now
where the time goes in v5:
time: 122 us
  Pallas kernels  120 us (98%)
  local copies, waits for them, and re-layouts  1.55 us (1%)
    pallas_call x1, Pallas kernels, front(): pl.pallas_call(front_kernel, out_shape=(jax.ShapeDtypeStruct((4, BLOCK, 2...  74.9 us
    pallas_call x1, Pallas kernels, back(): pl.pallas_call(back_kernel, out_shape=jax.ShapeDtypeStruct((48, 4096), jn...  27 us
    pallas_call x1, Pallas kernels, attend(): pl.pallas_call(attend_kernel, out_shape=jax.ShapeDtypeStruct((4, BLOCK, 2...  18.1 us

profile of v5, /device:TPU:10, one launch (start us, length us, event | category | flops | bytes accessed | tf_op | source)
XLA Modules:
  0.0 121.8 jit_solution(11314867914552297670)
XLA Ops:
  0.0 0.0 copy-start
  0.0 74.9 %front.1 = (bf16[4,192,256]{2,1,0:T(8,128)(2,1)}, bf16[2,4,4,4,192,128]{5,4,3,2,1,0:T(8,128)(2,1)}, s32[8,128]{1,0:T(8,128)}) custom-call(bf16[48,4096]{1,0:T(8,128)(2,1)} %hidden.1, f32[1,4096]{1,0:T(1,128)} %bitcast.5, bf16[256,1024]{1,0:T(8,128)(2,1)} %w_query.1, bf16[256,256]{1,0:T(8,128)(2,1)} %w_key.1, bf16[256,256]{1,0:T(8,128)(2,1)} %w_value.1, ...), custom_call_target="tpu_custom_call" | custom-call | tf_op jit(solution)/shard_map/front/pallas_call | solution.py:503
  75.0 0.7 reshape.136
  75.7 0.1 pad_add_fusion
  75.8 0.1 fusion.5
  75.8 0.1 stack.2.bounds
  75.9 18.1 %attend.1.own = bf16[4,192,256]{2,1,0:T(8,128)(2,1)S(1)} custom-call(s32[4,5]{1,0:T(4,128)S(1)} %stack.2.bounds, bf16[4,192,256]{2,1,0:T(8,128)(2,1)} %get-tuple-element.9.q_ref, bf16[2,4,4,4,192,128]{5,4,3,2,1,0:T(8,128)(2,1)} %get-tuple-element.10.both_in, s32[4,1,384]{2,1,0:T(1,128)S(1)} %reshape.137.first_ref), custom_call_target="tpu_custom_call" | custom-call | tf_op jit(solution)/shard_map/attend/pallas_call | solution.py:621
  94.0 0.0 copy-done
  94.1 27.0 %back.1 = bf16[48,4096]{1,0:T(8,128)(2,1)S(1)} custom-call(bf16[4,192,256]{2,1,0:T(8,128)(2,1)S(1)} %attend.1.own, bf16[1024,4096]{1,0:T(8,128)(2,1)} %w_out.1, bf16[48,4096]{1,0:T(8,128)(2,1)S(1)} %copy-done), custom_call_target="tpu_custom_call" | custom-call | tf_op jit(solution)/shard_map/back/pallas_call | solution.py:730
  121.0 0.7 copy.11
  (3 shorter events, 0.0 us)
Async XLA Ops:
  0.0 94.0 %copy-start = (bf16[48,4096]{1,0:T(8,128)(2,1)S(1)}, bf16[48,4096]{1,0:T(8,128)(2,1)}, u32[]{:S(2)}) copy-start(bf16[48,4096]{1,0:T(8,128)(2,1)} %hidden.1) | copy-start | bytes 1179652

commit v6 on v5

--- a/solution.py
+++ b/solution.py
@@ -484,7 +484,8 @@
         first = jnp.zeros((2, 128), jnp.float32)
         for d in range(1, 6):
             first = jnp.where(documents == d, firsts[d - 1], first)
-        first_out[2 * zb : 2 * zb + 2, :] = first.astype(jnp.int32)
+        first = first.astype(jnp.int32)
+        first_out[zb] = jnp.concatenate([first[0:1], first[1:2, :64]] * 2, axis=1)
     key_end(3)
     for copy in siblings:
         copy.wait_recv()
@@ -505,7 +506,7 @@
         out_shape=(
             jax.ShapeDtypeStruct((4, BLOCK, 2 * HEAD_SIZE), jnp.bfloat16),
             jax.ShapeDtypeStruct((2, 4, 4, 4, BLOCK, HEAD_SIZE), jnp.bfloat16),
-            jax.ShapeDtypeStruct((8, 128), jnp.int32),
+            jax.ShapeDtypeStruct((4, 1, 2 * BLOCK), jnp.int32),
         ),
         in_specs=[outside] * 8,
         out_specs=(outside, outside, inside),
@@ -643,7 +644,7 @@
 
 def back_kernel(
     own, w_out, hidden, out,
-    attended, weights, mine, given, landed, joined, arrived,
+    attended, weights, first, mine, given, landed, joined, arrived,
     send_sems, recv_sems, local_sems, step_send, step_recv,
 ):
     x, y, zh, zl, c = place()
@@ -681,7 +682,9 @@
         else:
             copy.start()
         copies.append(copy)
-    for j in range(2):
+    near = jnp.where(here, zh % 2, 1 - zh % 2)
+
+    def arrive(j):
         for cc in range(2):
             arrives = pltpu.make_async_remote_copy(
                 src_ref=own.at[0],
@@ -693,7 +696,19 @@
             )
             local = (zh == 2 * c + j) & (c == cc)
             pl.when(jnp.logical_not(local))(arrives.wait_recv)
+
+    def multiply(j, i):
+        half = pl.ds(pl.multiple_of(j * 512, 512), 512)
+        return jnp.dot(
+            attended[:, half], weights[half, cut(i)], preferred_element_type=jnp.float32
+        )
+
+    arrive(near)
     pl.when(here)(stay.wait)
+    for i in range(pieces):
+        fetch[i].wait()
+        first[i] = multiply(near, i)
+    arrive(1 - near)
 
     cp = Copies(step_send, step_recv)
     to_sibling, to_across = [], []
@@ -704,9 +719,7 @@
         to_across.append(cp.send(joined.at[i], arrived.at[i], across))
 
     for i in range(pieces):
-        fetch[i].wait()
-        term = jnp.dot(attended[...], weights[:, cut(i)], preferred_element_type=jnp.float32)
-        term = term.reshape(2, 2, 48, width)
+        term = (first[i] + multiply(1 - near, i)).reshape(2, 2, 48, width)
         mine[i] = jnp.where(c == 0, term[:, 0], term[:, 1])
         given[i] = jnp.where(c == 0, term[:, 1], term[:, 0]).astype(jnp.bfloat16)
         to_sibling.append(cp.send(given.at[i], landed.at[i], sibling))
@@ -735,6 +748,7 @@
         scratch_shapes=[
             pltpu.VMEM((BLOCK, 1024), jnp.bfloat16),
             pltpu.VMEM((1024, 4096), jnp.bfloat16),
+            pltpu.VMEM((4, BLOCK, 1024), jnp.float32),
             pltpu.VMEM((4, 2, 48, 1024), jnp.float32),
             pltpu.VMEM((4, 2, 48, 1024), jnp.bfloat16),
             pltpu.VMEM((4, 2, 48, 1024), jnp.bfloat16),
@@ -766,18 +780,16 @@
         positions.reshape(1, BLOCK),
         jnp.asarray([inverse + inverse], dtype=jnp.float32),
     )
-    first = first.reshape(4, 256)[:, :BLOCK]
     row0 = (x * 16 + jnp.arange(4, dtype=jnp.int32) * 4 + y) * BLOCK
-    t_low = first[:, 0] // KEY_TILE
+    t_low = first[:, 0, 0] // KEY_TILE
     t_edge = jnp.maximum((row0 + 1) // KEY_TILE, t_low)
-    t_clear = jnp.clip((first[:, -1] + KEY_TILE - 1) // KEY_TILE, t_low, t_edge)
+    t_clear = jnp.clip((first[:, 0, -1] + KEY_TILE - 1) // KEY_TILE, t_low, t_edge)
     t_high = (row0 + BLOCK - 1) // KEY_TILE + 1
     bounds = jnp.stack([t_low, t_clear, t_edge, t_high, row0], axis=1)
-    lanes = jnp.concatenate([first, first], axis=1).reshape(4, 1, 2 * BLOCK)
     queries, both, w_out = (
         pltpu.with_memory_space_constraint(a, pltpu.HBM) for a in (queries, both, w_out)
     )
-    attended = attend(bounds, queries, both, lanes)
+    attended = attend(bounds, queries, both, first)
     return back(attended, w_out, hidden_in)
 
 

time: 122 us -> 128 us (1.049)
  the two profiles are of different devices: /device:TPU:10 before, /device:TPU:46 now
where the time goes in v6:
time: 128 us; the launch traced here: 126 us
  Pallas kernels  123 us (96%)
  local copies, waits for them, and re-layouts  1.54 us (1%)
    pallas_call x1, Pallas kernels, front(): pl.pallas_call(front_kernel, out_shape=(jax.ShapeDtypeStruct((4, BLOCK, 2...  73 us
    pallas_call x1, Pallas kernels, back(): pl.pallas_call(back_kernel, out_shape=jax.ShapeDtypeStruct((48, 4096), jn...  27.2 us
    pallas_call x1, Pallas kernels, attend(): pl.pallas_call(attend_kernel, out_shape=jax.ShapeDtypeStruct((4, BLOCK, 2...  23.1 us

profile of v6, /device:TPU:46, one launch (start us, length us, event | category | flops | bytes accessed | tf_op | source)
XLA Modules:
  0.0 125.6 jit_solution(8431723934270216508)
XLA Ops:
  0.0 0.0 copy-start
  0.0 73.0 %front.1 = (bf16[4,192,256]{2,1,0:T(8,128)(2,1)}, bf16[2,4,4,4,192,128]{5,4,3,2,1,0:T(8,128)(2,1)}, s32[4,1,384]{2,1,0:T(1,128)}) custom-call(bf16[48,4096]{1,0:T(8,128)(2,1)} %hidden.1, f32[1,4096]{1,0:T(1,128)} %bitcast.5, bf16[256,1024]{1,0:T(8,128)(2,1)} %w_query.1, bf16[256,256]{1,0:T(8,128)(2,1)} %w_key.1, bf16[256,256]{1,0:T(8,128)(2,1)} %w_value.1, ...), custom_call_target="tpu_custom_call" | custom-call | tf_op jit(solution)/shard_map/front/pallas_call | solution.py:504
  73.0 0.8 slice_add_fusion
  73.8 0.1 stack.2.bounds
  73.9 0.0 copy-start.1
  73.9 0.7 copy-done.1
  74.6 23.1 %attend.1.own = bf16[4,192,256]{2,1,0:T(8,128)(2,1)S(1)} custom-call(s32[4,5]{1,0:T(4,128)S(1)} %stack.2.bounds, bf16[4,192,256]{2,1,0:T(8,128)(2,1)} %get-tuple-element.9.q_ref, bf16[2,4,4,4,192,128]{5,4,3,2,1,0:T(8,128)(2,1)} %get-tuple-element.10.both_in, s32[4,1,384]{2,1,0:T(1,128)S(1)} %copy-done.1), custom_call_target="tpu_custom_call" | custom-call | tf_op jit(solution)/shard_map/attend/pallas_call | solution.py:622
  97.7 0.0 copy-done
  97.7 27.2 %back.1 = bf16[48,4096]{1,0:T(8,128)(2,1)S(1)} custom-call(bf16[4,192,256]{2,1,0:T(8,128)(2,1)S(1)} %attend.1.own, bf16[1024,4096]{1,0:T(8,128)(2,1)} %w_out.1, bf16[48,4096]{1,0:T(8,128)(2,1)S(1)} %copy-done), custom_call_target="tpu_custom_call" | custom-call | tf_op jit(solution)/shard_map/back/pallas_call | solution.py:743
  124.9 0.7 copy.27
  (3 shorter events, 0.0 us)
Async XLA Ops:
  0.0 97.7 %copy-start = (bf16[48,4096]{1,0:T(8,128)(2,1)S(1)}, bf16[48,4096]{1,0:T(8,128)(2,1)}, u32[]{:S(2)}) copy-start(bf16[48,4096]{1,0:T(8,128)(2,1)} %hidden.1) | copy-start | bytes 1179652
  73.9 0.7 copy-start.1

commit v7 on v5

--- a/solution.py
+++ b/solution.py
@@ -348,126 +348,126 @@
         share(s, 2)
 
     scatter_weights(1)
+    ring_start(1)
+    own_start()
+    ring_start(0)
+    scatter_weights(0)
+    collect_weights(1)
+    along_x(1, 0)
     meta_start()
-    scatter_weights(0)
-    ring_start(0)
-    ring_start(1)
-    collect_weights(1)
     along_y(1)
-    along_x(1, 0)
     forward_y(1, 0)
-    own_start()
+    ring(0, 0, 0)
+    forward_y(1, 1)
     along_x(1, 3)
+    ring(0, 1, 0)
     collect_weights(0)
-    ring(0, 0, 0)
-    forward_x(1, 0, 1)
-    forward_y(1, 1)
     along_x(1, 1)
-    forward_x(1, 0, 0)
     along_y(0)
-    meta_along_y()
+    far_y(1)
     ring(0, 0, 1)
     forward_x(1, 3, 1)
-    far_y(1)
-    ring(0, 1, 0)
+    ring(0, 1, 1)
+    forward_x(1, 3, 0)
+    forward_x(1, 1, 1)
+    forward_x(1, 1, 0)
+    forward_x(1, 0, 0)
+    forward_x(1, 0, 1)
+    forward_x(1, 2, 1)
+    meta_along_y()
+    forward_y(0, 0)
+    forward_x(1, 2, 0)
+    ring(1, 0, 0)
     along_x(0, 0)
-    forward_x(1, 2, 0)
-    forward_x(1, 1, 0)
     forward_y(0, 1)
-    forward_x(1, 3, 0)
-    ring(1, 0, 0)
-    ring(0, 1, 1)
-    forward_x(1, 1, 1)
-    forward_x(1, 2, 1)
+    tables_of(order[0])
+    key_start(0)
+    along_x(0, 3)
+    ring(1, 0, 1)
+    ring(1, 1, 0)
+    ring(1, 1, 1)
+    tables_of(order[1])
+    key_x(0, 1)
     along_x(0, 1)
-    tables_of(order[0])
-    forward_y(0, 0)
-    ring(1, 0, 1)
-    tables_of(order[1])
-    key_start(0)
-    ring(1, 1, 0)
-    far_y(0)
-    along_x(0, 3)
     key_y(0, 0, 0)
+    key_x(0, 0)
+    key_start(1)
+    key_x_far(0)
+    forward_x(0, 3, 0)
     ring(2, 0, 0)
-    ring(1, 1, 1)
-    key_x(0, 0)
-    key_x(0, 1)
-    key_y(0, 0, 1)
-    key_start(1)
+    ring(2, 1, 0)
+    forward_x(0, 0, 1)
+    key_y(0, 3, 1)
+    tables_of(order[3])
+    ring(2, 0, 1)
     key_y(0, 3, 0)
-    ring(2, 1, 0)
-    forward_x(0, 3, 0)
-    forward_x(0, 1, 1)
-    ring(2, 0, 1)
-    key_y(0, 1, 1)
-    key_x_far(0)
     key_x(1, 0)
     key_x(1, 1)
+    forward_x(0, 0, 0)
+    forward_x(0, 1, 1)
+    tables_of(order[2])
+    key_y(0, 0, 1)
     ring(2, 1, 1)
+    key_y(1, 0, 1)
     key_y(0, 1, 0)
-    key_y(0, 3, 1)
-    key_y(1, 0, 1)
+    far_y(0)
+    key_x_far(1)
+    key_start(2)
+    key_y(1, 3, 0)
+    ring(3, 0, 1)
+    ring(3, 1, 0)
+    key_y(0, 2, 0)
+    key_y(1, 0, 0)
+    key_y(1, 1, 0)
+    key_y(0, 1, 1)
+    forward_x(0, 1, 0)
+    key_y(0, 2, 1)
+    forward_x(0, 3, 1)
+    key_y(1, 2, 1)
+    ring(3, 1, 1)
+    key_y(1, 1, 1)
     ring(3, 0, 0)
-    tables_of(order[2])
+    key_y(1, 3, 1)
+    forward_x(0, 2, 0)
     forward_x(0, 2, 1)
-    key_x_far(1)
-    key_y(0, 2, 0)
-    key_y(0, 2, 1)
-    forward_x(0, 1, 0)
-    key_y(1, 3, 0)
-    key_start(2)
-    forward_x(0, 0, 0)
-    key_y(1, 1, 0)
-    ring(3, 1, 0)
-    key_y(1, 3, 1)
-    ring(3, 1, 1)
     key_y(1, 2, 0)
-    forward_x(0, 3, 1)
-    key_y(1, 1, 1)
-    ring(3, 0, 1)
-    key_y(1, 2, 1)
-    key_y(1, 0, 0)
-    tables_of(order[3])
-    share(0, 1)
     key_x(2, 0)
+    share(1, 3)
+    share(0, 3)
     key_x(2, 1)
+    share(1, 1)
     key_start(3)
-    forward_x(0, 2, 0)
+    key_y(2, 0, 0)
     key_x_far(2)
     key_y(2, 0, 1)
-    forward_x(0, 0, 1)
+    key_x(3, 1)
+    key_x(3, 0)
+    key_end(0)
+    key_y(2, 3, 1)
+    share(0, 1)
+    key_y(2, 3, 0)
     key_end(1)
-    share(1, 1)
-    key_x(3, 0)
+    queries_of(1)
+    key_x_far(3)
+    queries_of(0)
+    key_y(3, 0, 0)
+    key_y(3, 0, 1)
+    key_y(2, 2, 0)
+    key_y(2, 1, 1)
     key_y(2, 1, 0)
-    key_x(3, 1)
-    share(1, 3)
-    key_end(0)
-    share(0, 3)
+    share(2, 3)
     key_y(2, 2, 1)
-    key_x_far(3)
-    key_y(2, 3, 1)
-    key_y(2, 0, 0)
-    key_y(2, 2, 0)
-    key_y(2, 3, 0)
-    key_y(2, 1, 1)
-    share(2, 3)
-    queries_of(2)
-    key_y(3, 0, 0)
+    share(2, 1)
     key_y(3, 3, 1)
-    queries_of(1)
-    share(2, 1)
+    key_y(3, 1, 0)
     key_y(3, 2, 0)
-    meta_along_x()
     key_y(3, 1, 1)
     key_y(3, 2, 1)
-    key_y(3, 0, 1)
-    key_y(3, 1, 0)
     key_y(3, 3, 0)
     share(3, 3)
     share(3, 1)
-    queries_of(0)
+    meta_along_x()
+    queries_of(2)
     key_end(2)
     queries_of(3)
     for copy in metas[2]:
@@ -651,7 +651,7 @@
     sibling, across = device(x, y, zh, zl, 1 - c), device(x, y, zh, 1 - zl, c)
     partners = [device(x, y, (zh + k) % 4, zl, cc) for k in range(4) for cc in (c, 1 - c)][1:]
     partners.append(across)
-    pieces = 4
+    pieces = 8
     width = 4096 // pieces
     cut = lambda i: pl.ds(i * width, width)
     fetch = [
@@ -735,16 +735,16 @@
         scratch_shapes=[
             pltpu.VMEM((BLOCK, 1024), jnp.bfloat16),
             pltpu.VMEM((1024, 4096), jnp.bfloat16),
-            pltpu.VMEM((4, 2, 48, 1024), jnp.float32),
-            pltpu.VMEM((4, 2, 48, 1024), jnp.bfloat16),
-            pltpu.VMEM((4, 2, 48, 1024), jnp.bfloat16),
-            pltpu.VMEM((4, 48, 1024), jnp.bfloat16),
-            pltpu.VMEM((4, 48, 1024), jnp.bfloat16),
+            pltpu.VMEM((8, 2, 48, 512), jnp.float32),
+            pltpu.VMEM((8, 2, 48, 512), jnp.bfloat16),
+            pltpu.VMEM((8, 2, 48, 512), jnp.bfloat16),
+            pltpu.VMEM((8, 48, 512), jnp.bfloat16),
+            pltpu.VMEM((8, 48, 512), jnp.bfloat16),
             pltpu.SemaphoreType.DMA((4,)),
             pltpu.SemaphoreType.DMA((4,)),
-            pltpu.SemaphoreType.DMA((5,)),
-            pltpu.SemaphoreType.DMA((8,)),
-            pltpu.SemaphoreType.DMA((8,)),
+            pltpu.SemaphoreType.DMA((9,)),
+            pltpu.SemaphoreType.DMA((16,)),
+            pltpu.SemaphoreType.DMA((16,)),
         ],
         compiler_params=pltpu.CompilerParams(
             collective_id=1, has_side_effects=True, vmem_limit_bytes=32 << 20

time: 122 us -> 131 us (1.074)
  the two profiles are of different devices: /device:TPU:10 before, /device:TPU:46 now
where the time goes in v7:
time: 131 us; the launch traced here: 130 us
  Pallas kernels  129 us (98%)
  local copies, waits for them, and re-layouts  1.55 us (1%)
    pallas_call x1, Pallas kernels, front(): pl.pallas_call(front_kernel, out_shape=(jax.ShapeDtypeStruct((4, BLOCK, 2...  74.4 us
    pallas_call x1, Pallas kernels, back(): pl.pallas_call(back_kernel, out_shape=jax.ShapeDtypeStruct((48, 4096), jn...  28.1 us
    pallas_call x1, Pallas kernels, attend(): pl.pallas_call(attend_kernel, out_shape=jax.ShapeDtypeStruct((4, BLOCK, 2...  26.1 us

profile of v7, /device:TPU:46, one launch (start us, length us, event | category | flops | bytes accessed | tf_op | source)
XLA Modules:
  0.0 130.4 jit_solution(7696143431067529713)
XLA Ops:
  0.0 0.0 copy-start
  0.0 74.4 %front.1 = (bf16[4,192,256]{2,1,0:T(8,128)(2,1)}, bf16[2,4,4,4,192,128]{5,4,3,2,1,0:T(8,128)(2,1)}, s32[8,128]{1,0:T(8,128)}) custom-call(bf16[48,4096]{1,0:T(8,128)(2,1)} %hidden.1, f32[1,4096]{1,0:T(1,128)} %bitcast.5, bf16[256,1024]{1,0:T(8,128)(2,1)} %w_query.1, bf16[256,256]{1,0:T(8,128)(2,1)} %w_key.1, bf16[256,256]{1,0:T(8,128)(2,1)} %w_value.1, ...), custom_call_target="tpu_custom_call" | custom-call | tf_op jit(solution)/shard_map/front/pallas_call | solution.py:503
  74.5 0.7 reshape.136
  75.1 0.1 pad_add_fusion
  75.2 0.1 fusion.5
  75.3 0.1 stack.2.bounds
  75.4 26.1 %attend.1.own = bf16[4,192,256]{2,1,0:T(8,128)(2,1)S(1)} custom-call(s32[4,5]{1,0:T(4,128)S(1)} %stack.2.bounds, bf16[4,192,256]{2,1,0:T(8,128)(2,1)} %get-tuple-element.9.q_ref, bf16[2,4,4,4,192,128]{5,4,3,2,1,0:T(8,128)(2,1)} %get-tuple-element.10.both_in, s32[4,1,384]{2,1,0:T(1,128)S(1)} %reshape.137.first_ref), custom_call_target="tpu_custom_call" | custom-call | tf_op jit(solution)/shard_map/attend/pallas_call | solution.py:621
  101.5 0.0 copy-done
  101.6 28.1 %back.1 = bf16[48,4096]{1,0:T(8,128)(2,1)S(1)} custom-call(bf16[4,192,256]{2,1,0:T(8,128)(2,1)S(1)} %attend.1.own, bf16[1024,4096]{1,0:T(8,128)(2,1)} %w_out.1, bf16[48,4096]{1,0:T(8,128)(2,1)S(1)} %copy-done), custom_call_target="tpu_custom_call" | custom-call | tf_op jit(solution)/shard_map/back/pallas_call | solution.py:730
  129.7 0.7 copy.11
  (3 shorter events, 0.0 us)
Async XLA Ops:
  0.0 101.5 %copy-start = (bf16[48,4096]{1,0:T(8,128)(2,1)S(1)}, bf16[48,4096]{1,0:T(8,128)(2,1)}, u32[]{:S(2)}) copy-start(bf16[48,4096]{1,0:T(8,128)(2,1)} %hidden.1) | copy-start | bytes 1179652

commit v8 on v5

--- a/solution.py
+++ b/solution.py
@@ -11,7 +11,7 @@
 HEAD_SIZE = 128
 BLOCK = 192
 SEQUENCE = 12288
-KEY_TILE = 1024
+KEY_TILE = 1536
 KEY_PIECE = 256
 MESH = pl.DeviceIdType.MESH
 FRONT_COPIES = 190
@@ -350,126 +350,126 @@
     scatter_weights(1)
     meta_start()
     scatter_weights(0)
-    ring_start(0)
     ring_start(1)
     collect_weights(1)
     along_y(1)
     along_x(1, 0)
+    ring_start(0)
     forward_y(1, 0)
-    own_start()
+    forward_y(1, 1)
     along_x(1, 3)
     collect_weights(0)
+    ring(0, 1, 0)
+    along_x(1, 1)
+    along_y(0)
+    far_y(1)
+    own_start()
+    along_x(0, 0)
+    ring(0, 1, 1)
+    forward_x(1, 1, 0)
+    forward_x(1, 3, 1)
     ring(0, 0, 0)
+    ring(0, 0, 1)
+    forward_x(1, 3, 0)
+    meta_along_y()
     forward_x(1, 0, 1)
-    forward_y(1, 1)
-    along_x(1, 1)
+    forward_x(1, 1, 1)
+    forward_y(0, 1)
+    forward_y(0, 0)
+    forward_x(1, 2, 1)
+    tables_of(order[0])
+    forward_x(1, 2, 0)
+    tables_of(order[1])
     forward_x(1, 0, 0)
-    along_y(0)
-    meta_along_y()
-    ring(0, 0, 1)
-    forward_x(1, 3, 1)
-    far_y(1)
-    ring(0, 1, 0)
-    along_x(0, 0)
-    forward_x(1, 2, 0)
-    forward_x(1, 1, 0)
-    forward_y(0, 1)
-    forward_x(1, 3, 0)
-    ring(1, 0, 0)
-    ring(0, 1, 1)
-    forward_x(1, 1, 1)
-    forward_x(1, 2, 1)
     along_x(0, 1)
-    tables_of(order[0])
-    forward_y(0, 0)
-    ring(1, 0, 1)
-    tables_of(order[1])
-    key_start(0)
     ring(1, 1, 0)
     far_y(0)
+    ring(1, 1, 1)
+    key_start(0)
+    tables_of(order[2])
+    ring(1, 0, 0)
+    ring(1, 0, 1)
     along_x(0, 3)
-    key_y(0, 0, 0)
-    ring(2, 0, 0)
-    ring(1, 1, 1)
     key_x(0, 0)
     key_x(0, 1)
+    tables_of(order[3])
+    forward_x(0, 1, 1)
+    ring(2, 1, 0)
+    key_start(1)
+    ring(2, 0, 0)
     key_y(0, 0, 1)
-    key_start(1)
+    ring(2, 1, 1)
+    forward_x(0, 2, 1)
+    key_y(0, 0, 0)
+    key_x_far(0)
+    ring(3, 1, 0)
+    key_y(0, 1, 0)
     key_y(0, 3, 0)
-    ring(2, 1, 0)
-    forward_x(0, 3, 0)
-    forward_x(0, 1, 1)
+    key_y(0, 3, 1)
+    forward_x(0, 1, 0)
+    forward_x(0, 2, 0)
+    key_y(1, 0, 1)
+    key_y(0, 1, 1)
+    key_x(1, 0)
     ring(2, 0, 1)
-    key_y(0, 1, 1)
-    key_x_far(0)
-    key_x(1, 0)
     key_x(1, 1)
-    ring(2, 1, 1)
-    key_y(0, 1, 0)
-    key_y(0, 3, 1)
-    key_y(1, 0, 1)
+    key_y(1, 0, 0)
     ring(3, 0, 0)
-    tables_of(order[2])
-    forward_x(0, 2, 1)
+    key_y(0, 2, 1)
+    ring(3, 1, 1)
+    key_start(2)
+    forward_x(0, 0, 1)
+    forward_x(0, 0, 0)
+    forward_x(0, 3, 1)
+    key_y(0, 2, 0)
+    key_y(1, 1, 0)
+    key_y(1, 3, 1)
     key_x_far(1)
-    key_y(0, 2, 0)
-    key_y(0, 2, 1)
-    forward_x(0, 1, 0)
-    key_y(1, 3, 0)
-    key_start(2)
-    forward_x(0, 0, 0)
-    key_y(1, 1, 0)
-    ring(3, 1, 0)
-    key_y(1, 3, 1)
-    ring(3, 1, 1)
-    key_y(1, 2, 0)
-    forward_x(0, 3, 1)
-    key_y(1, 1, 1)
     ring(3, 0, 1)
-    key_y(1, 2, 1)
-    key_y(1, 0, 0)
-    tables_of(order[3])
-    share(0, 1)
     key_x(2, 0)
     key_x(2, 1)
+    share(0, 3)
+    key_y(1, 3, 0)
+    forward_x(0, 3, 0)
+    share(0, 1)
     key_start(3)
-    forward_x(0, 2, 0)
+    key_y(1, 2, 1)
     key_x_far(2)
-    key_y(2, 0, 1)
-    forward_x(0, 0, 1)
-    key_end(1)
-    share(1, 1)
-    key_x(3, 0)
+    key_y(1, 1, 1)
+    key_y(1, 2, 0)
+    queries_of(3)
+    key_x(3, 1)
+    key_y(2, 3, 0)
     key_y(2, 1, 0)
-    key_x(3, 1)
     share(1, 3)
     key_end(0)
-    share(0, 3)
+    key_x(3, 0)
     key_y(2, 2, 1)
+    share(1, 1)
     key_x_far(3)
     key_y(2, 3, 1)
+    key_y(2, 2, 0)
+    key_y(2, 0, 1)
     key_y(2, 0, 0)
-    key_y(2, 2, 0)
-    key_y(2, 3, 0)
+    key_end(1)
+    key_y(3, 0, 1)
     key_y(2, 1, 1)
+    queries_of(0)
+    key_y(3, 0, 0)
     share(2, 3)
+    share(2, 1)
+    key_y(3, 3, 0)
+    key_y(3, 3, 1)
+    key_y(3, 1, 1)
+    key_y(3, 1, 0)
+    meta_along_x()
+    key_y(3, 2, 0)
+    share(3, 3)
+    key_y(3, 2, 1)
+    share(3, 1)
     queries_of(2)
-    key_y(3, 0, 0)
-    key_y(3, 3, 1)
+    key_end(2)
     queries_of(1)
-    share(2, 1)
-    key_y(3, 2, 0)
-    meta_along_x()
-    key_y(3, 1, 1)
-    key_y(3, 2, 1)
-    key_y(3, 0, 1)
-    key_y(3, 1, 0)
-    key_y(3, 3, 0)
-    share(3, 3)
-    share(3, 1)
-    queries_of(0)
-    key_end(2)
-    queries_of(3)
     for copy in metas[2]:
         copy.wait_recv()
     everything = meta[...].reshape(64, 8, 128)

time: 122 us -> 124 us (1.016)
  the two profiles are of different devices: /device:TPU:10 before, /device:TPU:36 now
where the time goes in v8:
time: 124 us
  Pallas kernels  122 us (98%)
  local copies, waits for them, and re-layouts  1.54 us (1%)
    pallas_call x1, Pallas kernels, front(): pl.pallas_call(front_kernel, out_shape=(jax.ShapeDtypeStruct((4, BLOCK, 2...  73.1 us
    pallas_call x1, Pallas kernels, back(): pl.pallas_call(back_kernel, out_shape=jax.ShapeDtypeStruct((48, 4096), jn...  27 us
    pallas_call x1, Pallas kernels, attend(): pl.pallas_call(attend_kernel, out_shape=jax.ShapeDtypeStruct((4, BLOCK, 2...  22 us

profile of v8, /device:TPU:36, one launch (start us, length us, event | category | flops | bytes accessed | tf_op | source)
XLA Modules:
  0.0 123.9 jit_solution(13613875347605066761)
XLA Ops:
  0.0 0.0 copy-start
  0.0 73.1 %front.1 = (bf16[4,192,256]{2,1,0:T(8,128)(2,1)}, bf16[2,4,4,4,192,128]{5,4,3,2,1,0:T(8,128)(2,1)}, s32[8,128]{1,0:T(8,128)}) custom-call(bf16[48,4096]{1,0:T(8,128)(2,1)} %hidden.1, f32[1,4096]{1,0:T(1,128)} %bitcast.5, bf16[256,1024]{1,0:T(8,128)(2,1)} %w_query.1, bf16[256,256]{1,0:T(8,128)(2,1)} %w_key.1, bf16[256,256]{1,0:T(8,128)(2,1)} %w_value.1, ...), custom_call_target="tpu_custom_call" | custom-call | tf_op jit(solution)/shard_map/front/pallas_call | solution.py:503
  73.1 0.7 reshape.94
  73.8 0.1 pad_add_fusion
  73.9 0.1 fusion.2
  74.0 0.1 stack.2.bounds
  74.1 22.0 %attend.1.own = bf16[4,192,256]{2,1,0:T(8,128)(2,1)S(1)} custom-call(s32[4,5]{1,0:T(4,128)S(1)} %stack.2.bounds, bf16[4,192,256]{2,1,0:T(8,128)(2,1)} %get-tuple-element.9.q_ref, bf16[2,4,4,4,192,128]{5,4,3,2,1,0:T(8,128)(2,1)} %get-tuple-element.10.both_in, s32[4,1,384]{2,1,0:T(1,128)S(1)} %reshape.95.first_ref), custom_call_target="tpu_custom_call" | custom-call | tf_op jit(solution)/shard_map/attend/pallas_call | solution.py:621
  96.1 0.0 copy-done
  96.2 27.0 %back.1 = bf16[48,4096]{1,0:T(8,128)(2,1)S(1)} custom-call(bf16[4,192,256]{2,1,0:T(8,128)(2,1)S(1)} %attend.1.own, bf16[1024,4096]{1,0:T(8,128)(2,1)} %w_out.1, bf16[48,4096]{1,0:T(8,128)(2,1)S(1)} %copy-done), custom_call_target="tpu_custom_call" | custom-call | tf_op jit(solution)/shard_map/back/pallas_call | solution.py:730
  123.2 0.7 copy.11
  (3 shorter events, 0.0 us)
Async XLA Ops:
  0.0 96.1 %copy-start = (bf16[48,4096]{1,0:T(8,128)(2,1)S(1)}, bf16[48,4096]{1,0:T(8,128)(2,1)}, u32[]{:S(2)}) copy-start(bf16[48,4096]{1,0:T(8,128)(2,1)} %hidden.1) | copy-start | bytes 1179652
